TPU v7x, 512 devices: a whole 4x8x8 slice. The times are simulated.
512 devices in a mesh: leaf: 128 (over z, y, core), rhs: 4 (over x).
Axes of the slice: x: 4, y: 8, z: 8, core: 2. Of those that a mesh axis runs over, the one named last changes fastest.
Arguments:
- potential: float32 [128, 1048576], P('rhs', 'leaf'), may hold values from -6 to 6
- geometry: float32 [4, 1048576], P(None, 'leaf'), as said below
- near_count: int32 [4096], P('leaf'), may hold values from 3 to 12, as said below
- near_offset: int32 [4096, 12], P('leaf'), may hold values from -6 to 6, as said below
- far_offset: int32 [4096, 4], P('leaf'), may hold values from -8 to 8, as said below
- col_basis: bfloat16 [4096, 256, 64], P('leaf'), may hold values from -0.375 to 0.375
- row_basis: bfloat16 [4096, 256, 64], P('leaf'), may hold values from -0.5 to 0.5
- leaf_up: bfloat16 [4096, 64, 64], P('leaf'), may hold values from -0.125 to 0.125
- leaf_down: bfloat16 [4096, 64, 64], P('leaf'), may hold values from -0.75 to 0.75
- leaf_coupling: bfloat16 [4096, 4, 64, 64], P('leaf'), may hold values from -0.375 to 0.375
- up_transfer: bfloat16 [2, 64, 64], replicated, may hold values from -0.5 to 0.5
- down_transfer: bfloat16 [2, 64, 64], replicated, may hold values from -0.75 to 0.75
- sibling_coupling: bfloat16 [2, 64, 64], replicated, may hold values from -0.375 to 0.375
Outputs:
- field: float32 [128, 1048576], P('rhs', 'leaf')
Inputs may be any that keep to these rules, and one draw needn't show every extreme that they name: `geometry`: rows 0 to 2 are panel centroids, row 3 panel areas between 0.005 and 0.05. Each leaf cluster uses slots 0 to near_count - 1; some cluster uses all 12. `near_offset`: slot 0 of every cluster is the cluster itself (offset 0), slot 1 holds a positive offset and slot 2 a negative one; the other slots of a cluster hold distinct nonzero offsets. `far_offset`: every offset has magnitude above 6; the offsets of one cluster are distinct.
All inputs are finite; a program needn't handle non-finite values.
Results may differ from a plain program's by a relative error of at most 0.007.
Values may be sent and summed in bfloat16 or wider, within the bound.
No kernel may reach another device: no remote copies, remote signals or barrier semaphores. Data moves between devices by JAX's collectives and lax.ppermute only.
A program may use at most 64 MiB of HBM per device.

v0:
```python
import math

import jax
import jax.numpy as jnp
from jax import lax
from jax.sharding import PartitionSpec as P

NNEAR = 12
NWIN = 6
FWIN = 8


def with_halo(value, sides, width):
    for axis, dim in sides:
        devices, length = (lax.axis_size(axis), value.shape[dim])
        up = [(i, (i + 1) % devices) for i in range(devices - 1)]
        down = [(j, i) for i, j in up]
        last = lax.slice_in_dim(value, length - width, length, axis=dim)
        first = lax.slice_in_dim(value, 0, width, axis=dim)
        before = lax.ppermute(last, axis, up)
        after = lax.ppermute(first, axis, down)
        value = jnp.concatenate([before, value, after], axis=dim)
    return value


def from_partner(value, axis, apart):
    return lax.ppermute(value, axis, [(i, i ^ 1 << apart) for i in range(lax.axis_size(axis))])


def kernel_entries(target_geometry, source_geometry):
    squared = (target_geometry[0][:, :, None] - source_geometry[0][:, None, :]) ** 2
    squared = squared + (target_geometry[1][:, :, None] - source_geometry[1][:, None, :]) ** 2
    squared = squared + (target_geometry[2][:, :, None] - source_geometry[2][:, None, :]) ** 2
    spread = (target_geometry[3][:, :, None] + source_geometry[3][:, None, :]) / math.pi
    return source_geometry[3][:, None, :] / jnp.sqrt(squared + spread)


def select_side(table, side_bit):
    return lax.dynamic_index_in_dim(table, side_bit, 0, keepdims=False)


def per_device(
    potential,
    geometry,
    near_count,
    near_offset,
    far_offset,
    col_basis,
    row_basis,
    leaf_up,
    leaf_down,
    leaf_coupling,
    up_transfer,
    down_transfer,
    sibling_coupling,
):
    rows_here = potential.shape[0]
    clusters = near_count.shape[0]
    panels = col_basis.shape[1]
    basis_rank = col_basis.shape[2]
    partners_count = far_offset.shape[1]
    column_parts = lax.axis_size("rhs")
    per_part = clusters // column_parts
    first_local = lax.axis_index("rhs") * per_part
    window_width = per_part + 2 * NWIN
    stacked = jnp.concatenate([potential, geometry], axis=0)
    extended = with_halo(stacked, (("leaf", 1),), NWIN * panels)
    wide_rows = extended.shape[1] // panels
    value_rows = extended[:rows_here].astype(jnp.bfloat16)
    sources = lax.all_gather(value_rows, "rhs", axis=0, tiled=True)
    sources = sources.reshape(rows_here * column_parts, wide_rows, panels)
    all_rows = sources.shape[0]
    wide_geometry = extended[rows_here:].reshape(4, wide_rows, panels)
    local_geometry = lax.dynamic_slice_in_dim(wide_geometry, first_local, window_width, 1)
    target_geometry = local_geometry[:, NWIN : NWIN + per_part]
    live_counts = lax.dynamic_slice_in_dim(near_count, first_local, per_part, 0)
    offsets = lax.dynamic_slice_in_dim(near_offset, first_local, per_part, 0)
    own_clusters = NWIN + jnp.arange(per_part, dtype=jnp.int32)

    def add_slot(slot_index, running):
        shift_now = lax.dynamic_index_in_dim(offsets, slot_index, 1, keepdims=False)
        window_index = own_clusters + shift_now
        source_geometry = jnp.take(local_geometry, window_index, axis=1)
        source_values = jnp.take(sources, window_index + first_local, axis=1)
        live_mask = (slot_index < live_counts).astype(jnp.float32)
        near_block = (
            kernel_entries(target_geometry, source_geometry) * live_mask[:, None, None]
        ).astype(jnp.bfloat16)
        return running + jnp.einsum(
            "rcs,cts->rct", source_values, near_block, preferred_element_type=jnp.float32
        )

    start_sum = jnp.zeros((all_rows, per_part, panels), jnp.float32)
    near_part = lax.fori_loop(0, NNEAR, add_slot, start_sum)
    near_field = lax.all_to_all(
        near_part.reshape(all_rows, per_part * panels).astype(jnp.bfloat16),
        "rhs",
        split_axis=0,
        concat_axis=1,
        tiled=True,
    ).astype(jnp.float32)
    own_values = potential.astype(jnp.bfloat16).reshape(rows_here, clusters, panels)
    coefficients = jnp.einsum(
        "rcp,cpk->rck", own_values, col_basis, preferred_element_type=jnp.float32
    ).astype(jnp.bfloat16)
    rim_coefs = with_halo(
        coefficients.reshape(rows_here, clusters * basis_rank), (("leaf", 1),), FWIN * basis_rank
    )
    rim_coefs = rim_coefs.reshape(rows_here, clusters + 2 * FWIN, basis_rank)
    partner_index = jnp.arange(clusters, dtype=jnp.int32)[:, None] + FWIN + far_offset
    partners = jnp.take(rim_coefs, partner_index.reshape(-1), axis=1).reshape(
        rows_here, clusters, partners_count, basis_rank
    )
    leaf_far = jnp.einsum(
        "rcmk,cmkj->rcj", partners, leaf_coupling, preferred_element_type=jnp.float32
    )
    device_coef = jnp.einsum(
        "rck,ckj->rj", coefficients, leaf_up, preferred_element_type=jnp.float32
    ).astype(jnp.bfloat16)
    levels = lax.axis_size("leaf").bit_length() - 1
    device_index = lax.axis_index("leaf")
    couplings = []
    side_bits = []
    current = device_coef
    for tree_level in range(levels):
        side_bit = device_index // 2**tree_level % 2
        sibling = from_partner(current, "leaf", tree_level)
        couplings.append(
            jnp.dot(
                sibling, select_side(sibling_coupling, side_bit), preferred_element_type=jnp.float32
            )
        )
        side_bits.append(side_bit)
        if tree_level + 1 < levels:
            upward = jnp.dot(
                current, select_side(up_transfer, side_bit), preferred_element_type=jnp.float32
            )
            upward = upward + jnp.dot(
                sibling, select_side(up_transfer, 1 - side_bit), preferred_element_type=jnp.float32
            )
            current = upward.astype(jnp.bfloat16)
    local_sum = jnp.zeros((rows_here, basis_rank), jnp.float32)
    for tree_level in reversed(range(levels)):
        step_down = select_side(down_transfer, side_bits[tree_level]).astype(jnp.float32)
        local_sum = couplings[tree_level] + jnp.dot(
            local_sum, step_down, precision=lax.Precision.HIGHEST
        )
    leaf_local = leaf_far + jnp.einsum(
        "rk,ckj->rcj", local_sum, leaf_down.astype(jnp.float32), precision=lax.Precision.HIGHEST
    )
    leaf_local = leaf_local.astype(jnp.bfloat16)
    far_field = jnp.einsum(
        "rck,cpk->rcp", leaf_local, row_basis, preferred_element_type=jnp.float32
    )
    return near_field + far_field.reshape(rows_here, clusters * panels)


def solution(mesh):
    placed = (
        P("rhs", "leaf"),
        P(None, "leaf"),
        P("leaf"),
        P("leaf", None),
        P("leaf", None),
        P("leaf", None, None),
        P("leaf", None, None),
        P("leaf", None, None),
        P("leaf", None, None),
        P("leaf", None, None, None),
        P(),
        P(),
        P(),
    )
    return jax.shard_map(
        per_device, mesh=mesh, in_specs=placed, out_specs=P("rhs", "leaf"), check_vma=False
    )
```

profile of v0, /device:TPU:6, one launch (start us, length us, event | category | flops | bytes accessed | tf_op | source)
XLA Modules:
  0.0 242.6 jit_solution(15858377557532260188)
XLA Ops:
  6.5 1.8 fusion.132
  9.3 1.9 collective-permute-start.4
  12.0 1.9 reshape.114
  13.9 1.4 fusion.133
  15.3 3.0 %collective-permute-start.2 = (bf16[32,512]{1,0:T(8,128)(2,1)}, bf16[32,512]{1,0:T(8,128)(2,1)}, u32[]{:S(2)}, u32[]{:S(2)}) collective-permute-start(bf16[32,512]{1,0:T(8,128)(2,1)} %get-tuple-element.250), channel_id=1, source_target_pairs={{0,4},{4,8},{8,12},{12,16},{16,20},{20,24},{24,28},{28,32},{32,36}... | collective-permute-start | bytes 98312 | tf_op jit(solution)/shard_map/ppermute | solution.py:20
  18.3 1.3 collective-permute-start.3
  19.6 0.9 constant_dynamic-update-slice_fusion
  21.3 3.8 %collective-permute-start = (f32[36,1536]{1,0:T(8,128)}, f32[36,1536]{1,0:T(8,128)}, u32[]{:S(2)}, u32[]{:S(2)}) collective-permute-start(f32[36,1536]{1,0:T(8,128)} %get-tuple-element.246), channel_id=1, source_target_pairs={{0,4},{4,8},{8,12},{12,16},{16,20},{20,24},{24,28},{28,32},{32,36}... | collective-permute-start | bytes 663560 | tf_op jit(solution)/shard_map/ppermute | solution.py:20
  25.2 1.3 collective-permute-start.1
  28.9 5.2 %collective-permute-start.5 = (bf16[32,64]{1,0:T(8,128)(2,1)S(1)}, bf16[32,64]{1,0:T(8,128)(2,1)S(1)}, u32[]{:S(2)}, u32[]{:S(2)}) collective-permute-start(bf16[32,64]{1,0:T(8,128)(2,1)S(1)} %fusion.24), channel_id=1, source_target_pairs={{0,8},{4,12},{8,0},{12,4},{16,24},{20,28},{24,16},{28,20},{32,40},... | collective-permute-start | bytes 12296 | tf_op jit(solution)/shard_map/ppermute | solution.py:27
  34.2 1.5 collective-permute-done.5
  35.9 4.9 %collective-permute-start.6 = (bf16[32,64]{1,0:T(8,128)(2,1)S(1)}, bf16[32,64]{1,0:T(8,128)(2,1)S(1)}, u32[]{:S(2)}, u32[]{:S(2)}) collective-permute-start(bf16[32,64]{1,0:T(8,128)(2,1)S(1)} %fusion.25), channel_id=1, source_target_pairs={{0,16},{4,20},{8,24},{12,28},{16,0},{20,4},{24,8},{28,12},{32,48},... | collective-permute-start | bytes 12296 | tf_op jit(solution)/shard_map/ppermute | solution.py:27
  40.9 1.5 collective-permute-done.6
  42.5 10.5 %collective-permute-start.7 = (bf16[32,64]{1,0:T(8,128)(2,1)S(1)}, bf16[32,64]{1,0:T(8,128)(2,1)S(1)}, u32[]{:S(2)}, u32[]{:S(2)}) collective-permute-start(bf16[32,64]{1,0:T(8,128)(2,1)S(1)} %fusion.26), channel_id=1, source_target_pairs={{0,32},{4,36},{8,40},{12,44},{16,48},{20,52},{24,56},{28,60},{32,0... | collective-permute-start | bytes 12296 | tf_op jit(solution)/shard_map/ppermute | solution.py:27
  53.1 1.5 collective-permute-done.7
  55.4 6.2 %collective-permute-start.8 = (bf16[32,64]{1,0:T(8,128)(2,1)}, bf16[32,64]{1,0:T(8,128)(2,1)}, u32[]{:S(2)}, u32[]{:S(2)}) collective-permute-start(bf16[32,64]{1,0:T(8,128)(2,1)} %fusion.27), channel_id=1, source_target_pairs={{0,64},{4,68},{8,72},{12,76},{16,80},{20,84},{24,88},{28,92},{32,9... | collective-permute-start | bytes 12296 | tf_op jit(solution)/shard_map/ppermute | solution.py:27
  62.4 2.4 %pad_maximum_fusion = f32[36,11264]{1,0:T(8,128)} fusion(f32[36,1536]{1,0:T(8,128)} %collective-permute-done.1, f32[36,8192]{1,0:T(8,128)S(1)} %constant_dynamic-update-slice_fusion, f32[36,1536]{1,0:T(8,128)} %collective-permute-done), kind=kLoop, calls=%fused_computation.41 | loop fusion | flops 811008 | bytes 3244032 | tf_op jit(solution)/shard_map/concatenate | solution.py:22
  64.8 2.4 slice.115
  68.1 6.1 %collective-permute-start.9 = (bf16[32,64]{1,0:T(8,128)(2,1)S(1)}, bf16[32,64]{1,0:T(8,128)(2,1)S(1)}, u32[]{:S(2)}, u32[]{:S(2)}) collective-permute-start(bf16[32,64]{1,0:T(8,128)(2,1)S(1)} %fusion.28), channel_id=1, source_target_pairs={{0,128},{4,132},{8,136},{12,140},{16,144},{20,148},{24,152},{28,15... | collective-permute-start | bytes 12296 | tf_op jit(solution)/shard_map/ppermute | solution.py:27
  74.3 1.5 collective-permute-done.9
  75.9 9.8 %collective-permute-start.10 = (bf16[32,64]{1,0:T(8,128)(2,1)S(1)}, bf16[32,64]{1,0:T(8,128)(2,1)S(1)}, u32[]{:S(2)}, u32[]{:S(2)}) collective-permute-start(bf16[32,64]{1,0:T(8,128)(2,1)S(1)} %fusion.29), channel_id=1, source_target_pairs={{0,256},{4,260},{8,264},{12,268},{16,272},{20,276},{24,280},{28,28... | collective-permute-start | bytes 12296 | tf_op jit(solution)/shard_map/ppermute | solution.py:27
  85.7 1.2 pad_clamp_fusion.2
  86.9 1.2 copy.48
  88.1 1.2 dynamic_slice.98
  93.0 0.9 gather_fusion.2
  93.9 2.1 convolution_bitcast_fusion.2
  96.1 1.7 slice.106
  97.8 1.0 reshape.111
  98.9 11.3 %all-gather.2.cloned.1.call-done = bf16[128,11264]{1,0:T(8,128)(2,1)} async-done(((bf16[32,11264]{1,0:T(8,128)(2,1)}), bf16[128,11264]{1,0:T(8,128)(2,1)}) %all-gather.2.cloned.1.call-update) | async-done | bytes 2883600 | tf_op jit(solution)/shard_map/all_gather | solution.py:70
  110.2 4.6 %copy.43 = bf16[128,11264]{0,1:T(8,128)(2,1)} copy(bf16[128,11264]{1,0:T(8,128)(2,1)} %all-gather.2.cloned.1.call-done) | data formatting | bytes 5767168 | tf_op jit(solution)/shard_map/all_gather | solution.py:70
  114.8 4.6 %copy.45 = bf16[128,44,256]{2,0,1:T(8,128)(2,1)} copy(bf16[128,44,256]{0,2,1:T(8,128)(2,1)} %bitcast.197) | data formatting | bytes 5767168
  119.3 96.9 %while.14 = (s32[]{:T(128)}, f32[128,8,256]{0,2,1:T(8,128)}, s32[8,12]{0,1:T(8,128)}, f32[4,20,256]{2,0,1:T(4,128)S(1)}, f32[4,8,256]{2,1,0:T(8,128)S(1)}, /*ind...) while((s32[]{:T(128)}, f32[128,8,256]{0,2,1:T(8,128)}, ...), condition=%wide.region_1.2_spmd.clone, body=%wide.region_0.1_spmd.clone.sunk | while | flops 142354592 | bytes 4071995 | solution.py:94
  120.8 2.4 gather_fusion.1
  123.2 2.9 %fusion.174 = f32[128,8,256]{0,2,1:T(8,128)} fusion(f32[128,8,256]{0,2,1:T(8,128)} %get-tuple-element.342, f32[8]{0:T(128)S(1)} %compare_convert_fusion.2, f32[8,256]{1,0:T(8,128)S(1)} %get-tuple-element.316, f32[8,256]{1,0:T(8,128)S(1)} %get-tuple-element.320, f32[8,256]{1,0:T(8,128)S(1)} %get-tuple-element.321, ...), kind=kOutput, calls=%fused_computation.6.clone.1 | convolution fusion | flops 142344192 | bytes 2687017 | tf_op jit(solution)/shard_map/while/body/eval_jaxpr/rcs,cts->rct/dot_general | solution.py:89
  127.6 2.4 gather_fusion.1
  130.0 4.3 %fusion.174 = f32[128,8,256]{0,2,1:T(8,128)} fusion(f32[128,8,256]{0,2,1:T(8,128)} %get-tuple-element.342, f32[8]{0:T(128)S(1)} %compare_convert_fusion.2, f32[8,256]{1,0:T(8,128)S(1)} %get-tuple-element.316, f32[8,256]{1,0:T(8,128)S(1)} %get-tuple-element.320, f32[8,256]{1,0:T(8,128)S(1)} %get-tuple-element.321, ...), kind=kOutput, calls=%fused_computation.6.clone.1 | convolution fusion | flops 142344192 | bytes 2687017 | tf_op jit(solution)/shard_map/while/body/eval_jaxpr/rcs,cts->rct/dot_general | solution.py:89
  135.8 2.4 gather_fusion.1
  138.2 4.3 %fusion.174 = f32[128,8,256]{0,2,1:T(8,128)} fusion(f32[128,8,256]{0,2,1:T(8,128)} %get-tuple-element.342, f32[8]{0:T(128)S(1)} %compare_convert_fusion.2, f32[8,256]{1,0:T(8,128)S(1)} %get-tuple-element.316, f32[8,256]{1,0:T(8,128)S(1)} %get-tuple-element.320, f32[8,256]{1,0:T(8,128)S(1)} %get-tuple-element.321, ...), kind=kOutput, calls=%fused_computation.6.clone.1 | convolution fusion | flops 142344192 | bytes 2687017 | tf_op jit(solution)/shard_map/while/body/eval_jaxpr/rcs,cts->rct/dot_general | solution.py:89
  144.0 2.4 gather_fusion.1
  146.4 4.3 %fusion.174 = f32[128,8,256]{0,2,1:T(8,128)} fusion(f32[128,8,256]{0,2,1:T(8,128)} %get-tuple-element.342, f32[8]{0:T(128)S(1)} %compare_convert_fusion.2, f32[8,256]{1,0:T(8,128)S(1)} %get-tuple-element.316, f32[8,256]{1,0:T(8,128)S(1)} %get-tuple-element.320, f32[8,256]{1,0:T(8,128)S(1)} %get-tuple-element.321, ...), kind=kOutput, calls=%fused_computation.6.clone.1 | convolution fusion | flops 142344192 | bytes 2687017 | tf_op jit(solution)/shard_map/while/body/eval_jaxpr/rcs,cts->rct/dot_general | solution.py:89
  152.1 2.4 gather_fusion.1
  154.6 4.3 %fusion.174 = f32[128,8,256]{0,2,1:T(8,128)} fusion(f32[128,8,256]{0,2,1:T(8,128)} %get-tuple-element.342, f32[8]{0:T(128)S(1)} %compare_convert_fusion.2, f32[8,256]{1,0:T(8,128)S(1)} %get-tuple-element.316, f32[8,256]{1,0:T(8,128)S(1)} %get-tuple-element.320, f32[8,256]{1,0:T(8,128)S(1)} %get-tuple-element.321, ...), kind=kOutput, calls=%fused_computation.6.clone.1 | convolution fusion | flops 142344192 | bytes 2687017 | tf_op jit(solution)/shard_map/while/body/eval_jaxpr/rcs,cts->rct/dot_general | solution.py:89
  160.3 2.4 gather_fusion.1
  162.8 4.3 %fusion.174 = f32[128,8,256]{0,2,1:T(8,128)} fusion(f32[128,8,256]{0,2,1:T(8,128)} %get-tuple-element.342, f32[8]{0:T(128)S(1)} %compare_convert_fusion.2, f32[8,256]{1,0:T(8,128)S(1)} %get-tuple-element.316, f32[8,256]{1,0:T(8,128)S(1)} %get-tuple-element.320, f32[8,256]{1,0:T(8,128)S(1)} %get-tuple-element.321, ...), kind=kOutput, calls=%fused_computation.6.clone.1 | convolution fusion | flops 142344192 | bytes 2687017 | tf_op jit(solution)/shard_map/while/body/eval_jaxpr/rcs,cts->rct/dot_general | solution.py:89
  168.5 2.4 gather_fusion.1
  171.0 4.3 %fusion.174 = f32[128,8,256]{0,2,1:T(8,128)} fusion(f32[128,8,256]{0,2,1:T(8,128)} %get-tuple-element.342, f32[8]{0:T(128)S(1)} %compare_convert_fusion.2, f32[8,256]{1,0:T(8,128)S(1)} %get-tuple-element.316, f32[8,256]{1,0:T(8,128)S(1)} %get-tuple-element.320, f32[8,256]{1,0:T(8,128)S(1)} %get-tuple-element.321, ...), kind=kOutput, calls=%fused_computation.6.clone.1 | convolution fusion | flops 142344192 | bytes 2687017 | tf_op jit(solution)/shard_map/while/body/eval_jaxpr/rcs,cts->rct/dot_general | solution.py:89
  176.7 2.4 gather_fusion.1
  179.1 4.3 %fusion.174 = f32[128,8,256]{0,2,1:T(8,128)} fusion(f32[128,8,256]{0,2,1:T(8,128)} %get-tuple-element.342, f32[8]{0:T(128)S(1)} %compare_convert_fusion.2, f32[8,256]{1,0:T(8,128)S(1)} %get-tuple-element.316, f32[8,256]{1,0:T(8,128)S(1)} %get-tuple-element.320, f32[8,256]{1,0:T(8,128)S(1)} %get-tuple-element.321, ...), kind=kOutput, calls=%fused_computation.6.clone.1 | convolution fusion | flops 142344192 | bytes 2687017 | tf_op jit(solution)/shard_map/while/body/eval_jaxpr/rcs,cts->rct/dot_general | solution.py:89
  184.9 2.4 gather_fusion.1
  187.3 4.3 %fusion.174 = f32[128,8,256]{0,2,1:T(8,128)} fusion(f32[128,8,256]{0,2,1:T(8,128)} %get-tuple-element.342, f32[8]{0:T(128)S(1)} %compare_convert_fusion.2, f32[8,256]{1,0:T(8,128)S(1)} %get-tuple-element.316, f32[8,256]{1,0:T(8,128)S(1)} %get-tuple-element.320, f32[8,256]{1,0:T(8,128)S(1)} %get-tuple-element.321, ...), kind=kOutput, calls=%fused_computation.6.clone.1 | convolution fusion | flops 142344192 | bytes 2687017 | tf_op jit(solution)/shard_map/while/body/eval_jaxpr/rcs,cts->rct/dot_general | solution.py:89
  193.1 2.4 gather_fusion.1
  195.5 4.3 %fusion.174 = f32[128,8,256]{0,2,1:T(8,128)} fusion(f32[128,8,256]{0,2,1:T(8,128)} %get-tuple-element.342, f32[8]{0:T(128)S(1)} %compare_convert_fusion.2, f32[8,256]{1,0:T(8,128)S(1)} %get-tuple-element.316, f32[8,256]{1,0:T(8,128)S(1)} %get-tuple-element.320, f32[8,256]{1,0:T(8,128)S(1)} %get-tuple-element.321, ...), kind=kOutput, calls=%fused_computation.6.clone.1 | convolution fusion | flops 142344192 | bytes 2687017 | tf_op jit(solution)/shard_map/while/body/eval_jaxpr/rcs,cts->rct/dot_general | solution.py:89
  201.3 2.4 gather_fusion.1
  203.7 4.3 %fusion.174 = f32[128,8,256]{0,2,1:T(8,128)} fusion(f32[128,8,256]{0,2,1:T(8,128)} %get-tuple-element.342, f32[8]{0:T(128)S(1)} %compare_convert_fusion.2, f32[8,256]{1,0:T(8,128)S(1)} %get-tuple-element.316, f32[8,256]{1,0:T(8,128)S(1)} %get-tuple-element.320, f32[8,256]{1,0:T(8,128)S(1)} %get-tuple-element.321, ...), kind=kOutput, calls=%fused_computation.6.clone.1 | convolution fusion | flops 142344192 | bytes 2687017 | tf_op jit(solution)/shard_map/while/body/eval_jaxpr/rcs,cts->rct/dot_general | solution.py:89
  209.5 2.4 gather_fusion.1
  211.9 4.3 %fusion.174 = f32[128,8,256]{0,2,1:T(8,128)} fusion(f32[128,8,256]{0,2,1:T(8,128)} %get-tuple-element.342, f32[8]{0:T(128)S(1)} %compare_convert_fusion.2, f32[8,256]{1,0:T(8,128)S(1)} %get-tuple-element.316, f32[8,256]{1,0:T(8,128)S(1)} %get-tuple-element.320, f32[8,256]{1,0:T(8,128)S(1)} %get-tuple-element.321, ...), kind=kOutput, calls=%fused_computation.6.clone.1 | convolution fusion | flops 142344192 | bytes 2687017 | tf_op jit(solution)/shard_map/while/body/eval_jaxpr/rcs,cts->rct/dot_general | solution.py:89
  216.2 1.3 convert_element_type.76
  218.0 1.0 convert_element_type.77
  219.0 6.5 %all-to-all-start = ((bf16[4,32,2048]{2,1,0:T(8,128)(2,1)}), bf16[4,32,2048]{2,1,0:T(8,128)(2,1)}, u32[]{:S(2)}, u32[]{:S(2)}) async-start(bf16[4,32,2048]{2,1,0:T(8,128)(2,1)} %convert_element_type.77), calls=%async_computation | async-start | bytes 1048576 | tf_op jit(solution)/shard_map/all_to_all | solution.py:95
  225.5 1.4 fusion.20
  226.9 1.5 convolution_bitcast_fusion.1
  228.5 4.9 %all-to-all-done = bf16[4,32,2048]{2,1,0:T(8,128)(2,1)} async-done(((bf16[4,32,2048]{2,1,0:T(8,128)(2,1)}), bf16[4,32,2048]{2,1,0:T(8,128)(2,1)}, u32[]{:S(2)}, u32[]{:S(2)}) %all-to-all-start) | async-done | bytes 524320 | tf_op jit(solution)/shard_map/all_to_all | solution.py:95
  233.4 1.1 convert_bitcast_fusion
  234.6 1.1 add.363
  (229 shorter events, 29.3 us)
Async XLA Ops:
  6.5 87.4 %copy-start = (bf16[32,4,64,64]{3,2,1,0:T(8,128)(2,1)S(1)}, bf16[32,4,64,64]{3,2,1,0:T(8,128)(2,1)}, u32[]{:S(2)}) copy-start(bf16[32,4,64,64]{3,2,1,0:T(8,128)(2,1)} %param.24) | copy-start | bytes 3145732
  6.5 103.7 %all-gather.2.cloned.1.call-start = ((), (), s32[]{:S(2)}) async-start(), calls=%async_computation.1 | async-start | bytes 3604480 | tf_op jit(solution)/shard_map/all_gather | solution.py:70
  6.5 2.0 copy-start.3
  6.5 2.4 copy-start.5
  9.0 17.6 %copy-start.13 = (s32[32,4]{0,1:T(4,128)S(1)}, s32[32,4]{0,1:T(4,128)}, u32[]{:S(2)}) copy-start(s32[32,4]{0,1:T(4,128)} %param.19) | copy-start | bytes 1540
  9.0 18.9 %copy-start.2 = (bf16[2,64,64]{2,1,0:T(8,128)(2,1)S(1)}, bf16[2,64,64]{2,1,0:T(8,128)(2,1)}, u32[]{:S(2)}) copy-start(bf16[2,64,64]{2,1,0:T(8,128)(2,1)} %param.25) | copy-start | bytes 49156
  9.0 19.0 %copy-start.6 = (bf16[2,64,64]{2,1,0:T(8,128)(2,1)S(1)}, bf16[2,64,64]{2,1,0:T(8,128)(2,1)}, u32[]{:S(2)}) copy-start(bf16[2,64,64]{2,1,0:T(8,128)(2,1)} %param.26) | copy-start | bytes 49156
  9.0 19.1 %copy-start.12 = (s32[32,12]{0,1:T(8,128)S(1)}, s32[32,12]{0,1:T(8,128)}, u32[]{:S(2)}) copy-start(s32[32,12]{0,1:T(8,128)} %param.18) | copy-start | bytes 4612
  9.3 19.5 %collective-permute-start.4 = (bf16[32,64]{1,0:T(8,128)(2,1)S(1)}, bf16[32,64]{1,0:T(8,128)(2,1)S(1)}, u32[]{:S(2)}, u32[]{:S(2)}) collective-permute-start(bf16[32,64]{1,0:T(8,128)(2,1)S(1)} %fusion.23), channel_id=1, source_target_pairs={{0,4},{4,0},{8,12},{12,8},{16,20},{20,16},{24,28},{28,24},{32,36},... | collective-permute-start | bytes 12296 | tf_op jit(solution)/shard_map/ppermute | solution.py:27
  15.3 76.5 %collective-permute-start.2 = (bf16[32,512]{1,0:T(8,128)(2,1)}, bf16[32,512]{1,0:T(8,128)(2,1)}, u32[]{:S(2)}, u32[]{:S(2)}) collective-permute-start(bf16[32,512]{1,0:T(8,128)(2,1)} %get-tuple-element.250), channel_id=1, source_target_pairs={{0,4},{4,8},{8,12},{12,16},{16,20},{20,24},{24,28},{28,32},{32,36}... | collective-permute-start | bytes 98312 | tf_op jit(solution)/shard_map/ppermute | solution.py:20
  18.3 73.5 %collective-permute-start.3 = (bf16[32,512]{1,0:T(8,128)(2,1)}, bf16[32,512]{1,0:T(8,128)(2,1)}, u32[]{:S(2)}, u32[]{:S(2)}) collective-permute-start(bf16[32,512]{1,0:T(8,128)(2,1)} %get-tuple-element.251), channel_id=1, source_target_pairs={{4,0},{8,4},{12,8},{16,12},{20,16},{24,20},{28,24},{32,28},{36,32}... | collective-permute-start | bytes 98312 | tf_op jit(solution)/shard_map/ppermute | solution.py:21
  21.3 41.1 %collective-permute-start = (f32[36,1536]{1,0:T(8,128)}, f32[36,1536]{1,0:T(8,128)}, u32[]{:S(2)}, u32[]{:S(2)}) collective-permute-start(f32[36,1536]{1,0:T(8,128)} %get-tuple-element.246), channel_id=1, source_target_pairs={{0,4},{4,8},{8,12},{12,16},{16,20},{20,24},{24,28},{28,32},{32,36}... | collective-permute-start | bytes 663560 | tf_op jit(solution)/shard_map/ppermute | solution.py:20
  25.2 37.2 %collective-permute-start.1 = (f32[36,1536]{1,0:T(8,128)}, f32[36,1536]{1,0:T(8,128)}, u32[]{:S(2)}, u32[]{:S(2)}) collective-permute-start(f32[36,1536]{1,0:T(8,128)} %get-tuple-element.247), channel_id=1, source_target_pairs={{4,0},{8,4},{12,8},{16,12},{20,16},{24,20},{28,24},{32,28},{36,32}... | collective-permute-start | bytes 663560 | tf_op jit(solution)/shard_map/ppermute | solution.py:21
  28.8 32.8 %copy-start.8 = (bf16[32,64]{1,0:T(8,128)(2,1)}, bf16[32,64]{1,0:T(8,128)(2,1)S(1)}, u32[]{:S(2)}) copy-start(bf16[32,64]{1,0:T(8,128)(2,1)S(1)} %collective-permute-done.4) | copy-start | bytes 12292
  28.9 6.8 %collective-permute-start.5 = (bf16[32,64]{1,0:T(8,128)(2,1)S(1)}, bf16[32,64]{1,0:T(8,128)(2,1)S(1)}, u32[]{:S(2)}, u32[]{:S(2)}) collective-permute-start(bf16[32,64]{1,0:T(8,128)(2,1)S(1)} %fusion.24), channel_id=1, source_target_pairs={{0,8},{4,12},{8,0},{12,4},{16,24},{20,28},{24,16},{28,20},{32,40},... | collective-permute-start | bytes 12296 | tf_op jit(solution)/shard_map/ppermute | solution.py:27
  35.9 6.5 %collective-permute-start.6 = (bf16[32,64]{1,0:T(8,128)(2,1)S(1)}, bf16[32,64]{1,0:T(8,128)(2,1)S(1)}, u32[]{:S(2)}, u32[]{:S(2)}) collective-permute-start(bf16[32,64]{1,0:T(8,128)(2,1)S(1)} %fusion.25), channel_id=1, source_target_pairs={{0,16},{4,20},{8,24},{12,28},{16,0},{20,4},{24,8},{28,12},{32,48},... | collective-permute-start | bytes 12296 | tf_op jit(solution)/shard_map/ppermute | solution.py:27
  42.5 12.1 %collective-permute-start.7 = (bf16[32,64]{1,0:T(8,128)(2,1)S(1)}, bf16[32,64]{1,0:T(8,128)(2,1)S(1)}, u32[]{:S(2)}, u32[]{:S(2)}) collective-permute-start(bf16[32,64]{1,0:T(8,128)(2,1)S(1)} %fusion.26), channel_id=1, source_target_pairs={{0,32},{4,36},{8,40},{12,44},{16,48},{20,52},{24,56},{28,60},{32,0... | collective-permute-start | bytes 12296 | tf_op jit(solution)/shard_map/ppermute | solution.py:27
  54.6 6.9 %copy-start.10 = (bf16[32,64]{1,0:T(8,128)(2,1)}, bf16[32,64]{1,0:T(8,128)(2,1)S(1)}, u32[]{:S(2)}) copy-start(bf16[32,64]{1,0:T(8,128)(2,1)S(1)} %collective-permute-done.7) | copy-start | bytes 12292
  55.4 11.9 %collective-permute-start.8 = (bf16[32,64]{1,0:T(8,128)(2,1)}, bf16[32,64]{1,0:T(8,128)(2,1)}, u32[]{:S(2)}, u32[]{:S(2)}) collective-permute-start(bf16[32,64]{1,0:T(8,128)(2,1)} %fusion.27), channel_id=1, source_target_pairs={{0,64},{4,68},{8,72},{12,76},{16,80},{20,84},{24,88},{28,92},{32,9... | collective-permute-start | bytes 12296 | tf_op jit(solution)/shard_map/ppermute | solution.py:27
  62.4 27.0 %copy-start.7 = (bf16[2,64,64]{2,1,0:T(8,128)(2,1)S(1)}, bf16[2,64,64]{2,1,0:T(8,128)(2,1)}, u32[]{:S(2)}) copy-start(bf16[2,64,64]{2,1,0:T(8,128)(2,1)} %param.27) | copy-start | bytes 49156
  64.8 26.0 %copy-start.11 = (bf16[32,64]{1,0:T(8,128)(2,1)S(1)}, bf16[32,64]{1,0:T(8,128)(2,1)}, u32[]{:S(2)}) copy-start(bf16[32,64]{1,0:T(8,128)(2,1)} %copy-done.10) | copy-start | bytes 12292
  64.8 26.9 %copy-start.9 = (bf16[32,64]{1,0:T(8,128)(2,1)S(1)}, bf16[32,64]{1,0:T(8,128)(2,1)}, u32[]{:S(2)}) copy-start(bf16[32,64]{1,0:T(8,128)(2,1)} %copy-done.8) | copy-start | bytes 12292
  64.8 27.0 %copy-start.4 = (bf16[32,2048]{1,0:T(8,128)(2,1)S(1)}, bf16[32,2048]{1,0:T(8,128)(2,1)}, u32[]{:S(2)}) copy-start(bf16[32,2048]{1,0:T(8,128)(2,1)} %reshape.114) | copy-start | bytes 393220
  68.1 7.7 %collective-permute-start.9 = (bf16[32,64]{1,0:T(8,128)(2,1)S(1)}, bf16[32,64]{1,0:T(8,128)(2,1)S(1)}, u32[]{:S(2)}, u32[]{:S(2)}) collective-permute-start(bf16[32,64]{1,0:T(8,128)(2,1)S(1)} %fusion.28), channel_id=1, source_target_pairs={{0,128},{4,132},{8,136},{12,140},{16,144},{20,148},{24,152},{28,15... | collective-permute-start | bytes 12296 | tf_op jit(solution)/shard_map/ppermute | solution.py:27
  75.9 13.4 %collective-permute-start.10 = (bf16[32,64]{1,0:T(8,128)(2,1)S(1)}, bf16[32,64]{1,0:T(8,128)(2,1)S(1)}, u32[]{:S(2)}, u32[]{:S(2)}) collective-permute-start(bf16[32,64]{1,0:T(8,128)(2,1)S(1)} %fusion.29), channel_id=1, source_target_pairs={{0,256},{4,260},{8,264},{12,268},{16,272},{20,276},{24,280},{28,28... | collective-permute-start | bytes 12296 | tf_op jit(solution)/shard_map/ppermute | solution.py:27
  114.8 4.6 %copy-start.14 = (s32[8]{0:T(128)S(1)}, s32[8]{0:T(128)}, u32[]{:S(2)}) copy-start(s32[8]{0:T(128)} %dynamic_slice.98) | copy-start | bytes 100
  218.0 7.6 %copy-start.1 = (f32[32,32,64]{2,0,1:T(8,128)S(1)}, f32[32,32,64]{2,0,1:T(8,128)}, u32[]{:S(2)}) copy-start(f32[32,32,64]{2,0,1:T(8,128)} %convolution_bitcast_fusion.2) | copy-start | bytes 786436
  219.0 14.4 %all-to-all-start = ((bf16[4,32,2048]{2,1,0:T(8,128)(2,1)}), bf16[4,32,2048]{2,1,0:T(8,128)(2,1)}, u32[]{:S(2)}, u32[]{:S(2)}) async-start(bf16[4,32,2048]{2,1,0:T(8,128)(2,1)} %convert_element_type.77), calls=%async_computation | async-start | bytes 1048576 | tf_op jit(solution)/shard_map/all_to_all | solution.py:95
Sparse Core Ops, SparseCore 0:
  67.4 42.8 all-gather.1
where the time goes:
time: 247 us; the launch traced here: 243 us
  local copies, waits for them, and re-layouts  62.7 us (25%)
  matrix products  62.2 us (25%)
  starting transfers between devices  60.4 us (24%)
  waiting for transfers between devices  22.1 us (9%)
  other arithmetic  20.4 us (8%)
  between operations  13.9 us (6%)
    dot_general x12, matrix products, add_slot(): jnp.einsum('rcs,cts->rct', source_values, near_block, preferred_element_t...  50.4 us
    ppermute x7, starting transfers between devices, from_partner(): lax.ppermute(value, axis, [(i, i ^ 1 << apart) for i in range(lax.axis_si...  44.5 us
    gather x12, local copies, waits for them, and re-layouts, add_slot(): source_values = jnp.take(sources, window_index + first_local, axis=1)  28.7 us
    all_gather x1, waiting for transfers between devices, per_device(): sources = lax.all_gather(value_rows, 'rhs', axis=0, tiled=True)  11.3 us
    reduce_and x12, other arithmetic, add_slot(): source_values = jnp.take(sources, window_index + first_local, axis=1)  8.28 us
    gather x12, local copies, waits for them, and re-layouts, add_slot(): source_geometry = jnp.take(local_geometry, window_index, axis=1)  6.92 us
    ppermute x2, starting transfers between devices, with_halo(): before = lax.ppermute(last, axis, up)  6.83 us
    all_to_all x1, starting transfers between devices, per_device(): lax.all_to_all(near_part.reshape(all_rows, per_part * panels).astype(jnp....  6.51 us
  transfers between devices with their start and end apart: 13, of which 6 were waited for; matrix products, arithmetic and copies ran while one was open for 13% of the time, Pallas kernels for 0%

commit v1 on v0

v1 whole, which is shorter than its diff:
```python
import math

import jax
import jax.numpy as jnp
from jax import lax
from jax.experimental import pallas as pl
from jax.experimental.pallas import tpu as pltpu
from jax.sharding import PartitionSpec as P

NWIN = 6
FWIN = 8
LANES = 256
F32 = jnp.float32
BF16 = jnp.bfloat16
NT = (((1,), (1,)), ((), ()))


def whole(shape):
    return pl.BlockSpec(shape, lambda *_: (0,) * len(shape))


def mm(left, right):
    return jnp.dot(left, right, preferred_element_type=F32)


def mm_nt(left, right):
    return lax.dot_general(left, right, NT, preferred_element_type=F32)


def span(cluster):
    start = cluster * LANES
    if not isinstance(start, int):
        start = pl.multiple_of(start, LANES)
    return pl.ds(start, LANES)


def pieces(value):
    high = value.astype(BF16)
    rest = value - high.astype(F32)
    middle = rest.astype(BF16)
    low = (rest - middle.astype(F32)).astype(BF16)
    return high, middle, low


def column(row):
    halves = [
        jnp.broadcast_to(row[:, at : at + 128], (128, 128)).T for at in range(0, LANES, 128)
    ]
    return jnp.concatenate(halves, axis=0)


def inverse_distance(columns, rows):
    parts = []
    for at in range(0, LANES, 128):
        row = rows[:, at : at + 128]
        dx = columns[0] - row[0:1]
        dy = columns[1] - row[1:2]
        dz = columns[2] - row[2:3]
        squared = dx * dx + dy * dy + dz * dz + (columns[3] + row[3:4])
        parts.append(lax.rsqrt(squared).astype(BF16))
    return jnp.concatenate(parts, axis=1)


def masked(values, bits, place):
    return (values.astype(F32) * ((bits >> place) & 1).astype(F32)).astype(BF16)


def halo_message(dens_edge, geo_edge, coefs):
    edge = NWIN * LANES
    split = [piece.astype(F32) for piece in pieces(geo_edge)]
    split = jnp.concatenate(split + [jnp.zeros((4, edge), F32)], axis=0)
    wide = FWIN * 64
    coef_rows = jnp.concatenate(coefs, axis=1)
    below = jnp.concatenate([split, jnp.zeros((16, wide), F32)], axis=1).astype(BF16)
    above = jnp.concatenate([dens_edge, coef_rows], axis=1)
    return jnp.concatenate([above, below], axis=0)


def first_kernel(
    pot, geo, count, offset, basis, up, dens, scaled, coef, top, down_msg, up_msg, bits, total
):
    step = pl.program_id(0)
    steps = pl.num_programs(0)
    per_step = basis.shape[0]
    geometry = jnp.concatenate([geo[0:3, :], geo[3:4, :] * (1.0 / math.pi)], axis=0)
    scaled[...] = geometry
    coefs = []
    raised = None
    for local in range(per_step):
        rounded = pot[:, span(local)].astype(BF16)
        dens[:, span(local)] = (rounded.astype(F32) * geo[3:4, span(local)]).astype(BF16)
        value = mm_nt(rounded, basis[local]).astype(BF16)
        coef[local] = value
        coefs.append(value)
        product = mm(value, up[local])
        raised = product if raised is None else raised + product

    @pl.when(step == 0)
    def _():
        total[...] = raised
        slots = lax.broadcasted_iota(jnp.int32, offset.shape, 0)
        live = jnp.where(slots < count[...], jnp.left_shift(1, offset[...] + NWIN), 0)
        bits[...] = jnp.sum(live, axis=0, keepdims=True)
        edge = NWIN * LANES
        down_msg[...] = halo_message(dens[:, :edge], geometry[:, :edge], coefs)

    @pl.when(step > 0)
    def _():
        total[...] += raised

    @pl.when(step == steps - 1)
    def _():
        edge = (per_step - NWIN) * LANES
        up_msg[...] = halo_message(dens[:, edge:], geometry[:, edge:], coefs)
        packed = total[...]
        packed = jnp.concatenate([packed[:16], packed[16:]], axis=1).astype(BF16)
        for peer in range(top.shape[0]):
            top[peer] = packed


def near_kernel(first, last, bits, dens, geo, *refs):
    start, (out, held_a, held_b) = refs[:-3], refs[-3:]
    clusters = dens.shape[1] // LANES

    def prepare(cluster, held):
        rows = geo[:, span(jnp.minimum(cluster, clusters - 1))]
        for k in range(4):
            held[k] = column(rows[k : k + 1])

    def sweep(cluster, held, ahead):
        columns = [held.at[k][...] for k in range(4)]
        own = dens[:, span(cluster)]
        total = None
        for d in range(ahead):
            block = inverse_distance(columns, geo[:, span(cluster + d)])
            if d == 0:
                total = mm_nt(own, block)
                continue
            source = masked(dens[:, span(cluster + d)], bits[0, cluster], NWIN + d)
            total = total + mm_nt(source, block)
            back = masked(own, bits[0, cluster + d], NWIN - d)
            out[:, span(cluster + d)] += mm(back, block)
        out[:, span(cluster)] += total

    if first == 0:
        out[...] = jnp.zeros_like(out)
    else:
        out[...] = start[0][...]
    prepare(first, held_a)

    def pair(index, carry):
        cluster = first + index * 2
        prepare(cluster + 1, held_b)
        sweep(cluster, held_a, NWIN + 1)
        prepare(cluster + 2, held_a)
        sweep(cluster + 1, held_b, NWIN + 1)
        return carry

    full = (min(last, clusters - NWIN) - first) // 2
    lax.fori_loop(0, full, pair, 0)
    for cluster in range(first + full * 2, last):
        now, later = (held_a, held_b) if (cluster - first) % 2 == 0 else (held_b, held_a)
        if cluster + 1 < last:
            prepare(cluster + 1, later)
        sweep(cluster, now, min(NWIN + 1, clusters - cluster))


def side_by_side(one):
    zero = jnp.zeros((64, 64), BF16)
    return jnp.concatenate(
        [jnp.concatenate([one, zero], axis=1), jnp.concatenate([zero, one], axis=1)], axis=0
    )


def climb(current, up, place, nodes, top):
    sides = [side_by_side(up[side]) for side in range(2)]
    levels = (current.shape[0] // 16).bit_length() - 1
    siblings = []
    for level in range(levels):
        count = current.shape[0] // 16
        nodes[0 : count * 16] = current
        other = (place >> level) ^ 1
        siblings.append(nodes[pl.ds(pl.multiple_of(other * 16, 16), 16), :])
        if top or level + 1 < levels:
            paired = current.reshape(count // 2, 2, 16, 128)
            left = paired[:, 0].reshape(count * 8, 128)
            right = paired[:, 1].reshape(count * 8, 128)
            current = (mm(left, sides[0]) + mm(right, sides[1])).astype(BF16)
    return jnp.concatenate(siblings, axis=1), current


def middle_kernel(place, tops, up, siblings, spread, nodes):
    group = tops.shape[0] // 16
    siblings[...], root = climb(tops[...], up, place[0] & (group - 1), nodes, True)
    for peer in range(spread.shape[0]):
        spread[peer] = root


def last_kernel(
    bits,
    far,
    place,
    near,
    dens,
    geo,
    below,
    above,
    low_siblings,
    tops,
    coef,
    coupling,
    leaf_down,
    basis,
    up,
    down,
    sibling,
    out,
    window,
    weights_high,
    weights_low,
    nodes,
):
    clusters = coef.shape[0]
    levels = weights_high.shape[0] // 128
    device = place[0]
    edge = NWIN * LANES

    for j in range(FWIN):
        lanes = slice(edge + j * 64, edge + (j + 1) * 64)
        window[j] = below[0:32, lanes]
        window[FWIN + clusters + j] = above[0:32, lanes]
    window[FWIN : FWIN + clusters] = coef[...]

    weights_high[...] = jnp.zeros_like(weights_high)
    weights_low[...] = jnp.zeros_like(weights_low)
    path = None
    for level in range(levels):
        side = (device >> level) & 1
        coupled = sibling[side]
        if path is None:
            weight = coupled.astype(F32)
            path = down[side].astype(F32)
        else:
            high, middle, low = pieces(path)
            weight = mm(coupled, high) + mm(coupled, middle) + mm(coupled, low)
            step_down = down[side]
            path = mm(step_down, high) + mm(step_down, middle) + mm(step_down, low)
        high, middle, _ = pieces(weight)
        for at in (0, 64):
            rows = slice(level * 128 + at, level * 128 + at + 64)
            weights_high[rows, at : at + 64] = high
            weights_low[rows, at : at + 64] = middle

    below_levels = low_siblings.shape[1] // 128
    high_siblings, _ = climb(tops[...], up, device >> below_levels, nodes, False)
    stacked = jnp.concatenate([low_siblings[...], high_siblings], axis=1)
    packed = mm(stacked, weights_high[...]) + mm(stacked, weights_low[...])
    local = jnp.concatenate([packed[:, :64], packed[:, 64:]], axis=0)
    local_high, local_low, _ = pieces(local)

    outer = [msg[32:48, :edge].astype(F32) for msg in (below, above)]
    outer = [part[0:4] + part[4:8] + part[8:12] for part in outer]
    for i in range(NWIN):
        for target, msg, geometry, sources in (
            (i, below, outer[0], range(i, NWIN)),
            (clusters - NWIN + i, above, outer[1], range(i + 1)),
        ):
            rows = geo[:, span(target)]
            columns = [column(rows[k : k + 1]) for k in range(4)]
            total = near[:, span(target)]
            for j in sources:
                apart = (j - NWIN if msg is below else clusters + j) - target
                lanes = slice(j * LANES, (j + 1) * LANES)
                block = inverse_distance(columns, geometry[:, lanes])
                source = masked(msg[0:32, lanes], bits[0, target], NWIN + apart)
                total = total + mm_nt(source, block)
            out[:, span(target)] = total
    for cluster in range(NWIN, clusters - NWIN):
        out[:, span(cluster)] = near[:, span(cluster)]

    unroll = 4

    def group(index, carry):
        for k in range(unroll):
            cluster = index * unroll + k
            partners = [window[cluster + FWIN + far[m, cluster]] for m in range(4)]
            partners = jnp.concatenate(partners, axis=1)
            total = mm(partners, coupling[cluster])
            step_down = leaf_down[cluster]
            total = total + (mm(local_high, step_down) + mm(local_low, step_down))
            out[:, span(cluster)] += mm(total.astype(BF16), basis[cluster])
        return carry

    lax.fori_loop(0, clusters // unroll, group, 0)


def per_device(
    potential,
    geometry,
    near_count,
    near_offset,
    far_offset,
    col_basis,
    row_basis,
    leaf_up,
    leaf_down,
    leaf_coupling,
    up_transfer,
    down_transfer,
    sibling_coupling,
):
    rows, width = potential.shape
    clusters, panels, rank = col_basis.shape
    per_step = FWIN
    params = pltpu.CompilerParams(vmem_limit_bytes=56 * 2**20)
    shape = jax.ShapeDtypeStruct
    lanes = per_step * panels
    message = (48, NWIN * panels + FWIN * rank)
    devices = lax.axis_size("leaf")
    levels = devices.bit_length() - 1
    outer = 2 ** (levels // 2)
    inner = devices // outer
    dens, scaled, coef, top, down_msg, up_msg, bits = pl.pallas_call(
        first_kernel,
        grid=(clusters // per_step,),
        in_specs=[
            pl.BlockSpec((rows, lanes), lambda i: (0, i)),
            pl.BlockSpec((4, lanes), lambda i: (0, i)),
            whole((1, clusters)),
            whole((near_offset.shape[1], clusters)),
            pl.BlockSpec((per_step, rank, panels), lambda i: (i, 0, 0)),
            pl.BlockSpec((per_step, rank, rank), lambda i: (i, 0, 0)),
        ],
        out_specs=[
            pl.BlockSpec((rows, lanes), lambda i: (0, i)),
            pl.BlockSpec((4, lanes), lambda i: (0, i)),
            pl.BlockSpec((per_step, rows, rank), lambda i: (i, 0, 0)),
            whole((inner, 16, 128)),
            whole(message),
            whole(message),
            whole((1, clusters)),
        ],
        out_shape=[
            shape((rows, width), BF16),
            shape((4, width), F32),
            shape((clusters, rows, rank), BF16),
            shape((inner, 16, 128), BF16),
            shape(message, BF16),
            shape(message, BF16),
            shape((1, clusters), jnp.int32),
        ],
        scratch_shapes=[pltpu.VMEM((rows, rank), F32)],
        compiler_params=params,
        name="first",
    )(
        potential,
        geometry,
        near_count.reshape(1, clusters),
        near_offset.T,
        col_basis.transpose(0, 2, 1),
        leaf_up,
    )
    upward = [(i, i + 1) for i in range(devices - 1)]
    downward = [(j, i) for i, j in upward]
    near_groups = [[at * inner + i for i in range(inner)] for at in range(outer)]
    far_groups = [[at * inner + i for at in range(outer)] for i in range(inner)]
    place = lax.axis_index("leaf").reshape(1).astype(jnp.int32)
    tops = lax.all_to_all(top, "leaf", 0, 0, axis_index_groups=near_groups)
    below = lax.ppermute(up_msg, "leaf", upward)
    above = lax.ppermute(down_msg, "leaf", downward)

    def near_part(first, last, *start):
        operands = (dens, scaled, *start)
        return pl.pallas_call(
            lambda *refs: near_kernel(first, last, *refs),
            grid_spec=pltpu.PrefetchScalarGridSpec(
                num_scalar_prefetch=1,
                grid=(1,),
                in_specs=[whole(x.shape) for x in operands],
                out_specs=whole((rows, width)),
                scratch_shapes=[pltpu.VMEM((4, panels, 128), F32)] * 2,
            ),
            out_shape=shape((rows, width), F32),
            compiler_params=params,
            cost_estimate=pl.CostEstimate(
                flops=(last - first) * 10**9 // 2,
                transcendentals=(last - first) * 7 * 65536,
                bytes_accessed=2 * 10**6,
            ),
            name="near",
        )(bits, *operands)

    cut = 12
    near = near_part(0, cut)
    tops, near = lax.optimization_barrier((tops, near))
    low_siblings, spread = pl.pallas_call(
        middle_kernel,
        grid_spec=pltpu.PrefetchScalarGridSpec(
            num_scalar_prefetch=1,
            grid=(1,),
            in_specs=[whole((inner * 16, 128)), whole(up_transfer.shape)],
            out_specs=[whole((16, (inner.bit_length() - 1) * 128)), whole((outer, 16, 128))],
            scratch_shapes=[pltpu.VMEM((inner * 16, 128), BF16)],
        ),
        out_shape=[
            shape((16, (inner.bit_length() - 1) * 128), BF16),
            shape((outer, 16, 128), BF16),
        ],
        compiler_params=params,
        name="middle",
    )(place, tops.reshape(inner * 16, 128), up_transfer)
    tops = lax.all_to_all(spread, "leaf", 0, 0, axis_index_groups=far_groups)
    near = near_part(cut, clusters, near, low_siblings)
    operands = (
        near,
        dens,
        scaled,
        below,
        above,
        low_siblings,
        tops.reshape(outer * 16, 128),
        coef,
        leaf_coupling.reshape(clusters, 4 * rank, rank),
        leaf_down,
        row_basis.transpose(0, 2, 1),
        up_transfer,
        down_transfer,
        sibling_coupling,
    )
    return pl.pallas_call(
        last_kernel,
        grid_spec=pltpu.PrefetchScalarGridSpec(
            num_scalar_prefetch=3,
            grid=(1,),
            in_specs=[whole(x.shape) for x in operands],
            out_specs=whole((rows, width)),
            scratch_shapes=[
                pltpu.VMEM((clusters + 2 * FWIN, rows, rank), BF16),
                pltpu.VMEM((levels * 128, 128), BF16),
                pltpu.VMEM((levels * 128, 128), BF16),
                pltpu.VMEM((outer * 16, 128), BF16),
            ],
        ),
        out_shape=shape((rows, width), F32),
        compiler_params=params,
        name="last",
    )(bits, far_offset.T, place, *operands)


def solution(mesh):
    placed = (
        P("rhs", "leaf"),
        P(None, "leaf"),
        P("leaf"),
        P("leaf", None),
        P("leaf", None),
        P("leaf", None, None),
        P("leaf", None, None),
        P("leaf", None, None),
        P("leaf", None, None),
        P("leaf", None, None, None),
        P(),
        P(),
        P(),
    )
    return jax.shard_map(
        per_device, mesh=mesh, in_specs=placed, out_specs=P("rhs", "leaf"), check_vma=False
    )
```

time: 247 us -> 80.1 us (0.32); the launches traced: 243 us -> 79.6 us
  matrix products: 62.2 us -> 0 us
  local copies, waits for them, and re-layouts: 62.7 us -> 1.38 us
  Pallas kernels: 0 us -> 51.8 us
  starting transfers between devices: 60.4 us -> 26.4 us
  waiting for transfers between devices: 22.1 us -> 0.01 us
  other arithmetic: 20.4 us -> 0 us
  between operations: 13.9 us -> 0.06 us
    dot_general x43 -> x0, matrix products: 62.2 us -> none  [the longest x12 50.4 us: add_slot(): jnp.einsum('rcs,cts->rct', source_values, near_block, preferred_element_t...]
    pallas_call x0 -> x5, Pallas kernels: none -> 51.8 us  [the longest x2 29.5 us: near_part(): pl.pallas_call(lambda *refs: near_kernel(first, last, *refs), grid_spec=p...]
    ppermute x11 -> x2, starting transfers between devices: 53.9 us -> 3.61 us  [the longest x1 2.31 us: per_device(): below = lax.ppermute(up_msg, 'leaf', upward)]
    gather x25 -> x0, local copies, waits for them, and re-layouts: 36.5 us -> none  [the longest x12 28.7 us: add_slot(): source_values = jnp.take(sources, window_index + first_local, axis=1)]
    all_to_all x1 -> x2, starting transfers between devices: 6.51 us -> 22.8 us  [the longest x1 15.6 us: per_device(): tops = lax.all_to_all(spread, 'leaf', 0, 0, axis_index_groups=far_groups)]
    all_gather x1 -> x0, waiting for transfers between devices: 11.3 us -> none  [per_device(): sources = lax.all_gather(value_rows, 'rhs', axis=0, tiled=True)]
    reduce_and x24 -> x0, other arithmetic: 8.38 us -> none  [the longest x12 8.28 us: add_slot(): source_values = jnp.take(sources, window_index + first_local, axis=1)]
    slice x17 -> x0, local copies, waits for them, and re-layouts: 6.58 us -> none  [the longest x1 2.36 us: per_device(): value_rows = extended[:rows_here].astype(jnp.bfloat16)]
  transfers between devices with their start and end apart: 13 -> 4, of which waited for: 6 -> 0; matrix products, arithmetic and copies ran while one was open for 13% -> 0% of each run, Pallas kernels for 0% -> 40%
where the time goes in v1:
time: 80.1 us; the launch traced here: 79.6 us
  Pallas kernels  51.8 us (65%)
  starting transfers between devices  26.4 us (33%)
  local copies, waits for them, and re-layouts  1.38 us (2%)
    pallas_call x2, Pallas kernels, near_part(): pl.pallas_call(lambda *refs: near_kernel(first, last, *refs), grid_spec=p...  29.5 us
    all_to_all x1, starting transfers between devices, per_device(): tops = lax.all_to_all(spread, 'leaf', 0, 0, axis_index_groups=far_groups)  15.6 us
    pallas_call x1, Pallas kernels, per_device(): pl.pallas_call(last_kernel, grid_spec=pltpu.PrefetchScalarGridSpec(num_sc...  15.5 us
    all_to_all x1, starting transfers between devices, per_device(): tops = lax.all_to_all(top, 'leaf', 0, 0, axis_index_groups=near_groups)  7.22 us
    pallas_call x1, Pallas kernels, per_device(): pl.pallas_call(first_kernel, grid=(clusters // per_step,), in_specs=[pl.B...  4.81 us
    ppermute x1, starting transfers between devices, per_device(): below = lax.ppermute(up_msg, 'leaf', upward)  2.31 us
    pallas_call x1, Pallas kernels, per_device(): pl.pallas_call(middle_kernel, grid_spec=pltpu.PrefetchScalarGridSpec(num_...  2.06 us
  transfers between devices with their start and end apart: 4, of which 0 were waited for; matrix products, arithmetic and copies ran while one was open for 0% of the time, Pallas kernels for 40%

profile of v1, /device:TPU:6, one launch (start us, length us, event | category | flops | bytes accessed | tf_op | source)
XLA Modules:
  0.0 79.6 jit_solution(5782897067357483183)
XLA Ops:
  0.0 4.8 %first.1 = (bf16[32,8192]{1,0:T(8,128)(2,1)}, f32[4,8192]{1,0:T(4,128)}, bf16[32,32,64]{2,1,0:T(8,128)(2,1)}, bf16[16,16,128]{2,1,0:T(8,128)(2,1)}, bf16[48,2048...) custom-call(f32[32,8192]{1,0:T(8,128)} %pot.1, f32[4,8192]{1,0:T(4,128)} %geo.1, s32[1,32]{1,0:T(1,128)} %bitcast.16, ...), custom_call_target="tpu_custom_call" | custom-call | tf_op jit(solution)/shard_map/first/pallas_call | solution.py:323
  4.8 7.2 %all-to-all-start = ((bf16[16,16,128]{2,1,0:T(8,128)(2,1)}), bf16[16,16,128]{2,1,0:T(8,128)(2,1)S(1)}, u32[]{:S(2)}, u32[]{:S(2)}) async-start(bf16[16,16,128]{2,1,0:T(8,128)(2,1)} %get-tuple-element.19), calls=%async_computation | async-start | bytes 131072 | tf_op jit(solution)/shard_map/all_to_all | solution.py:368
  12.0 2.3 %collective-permute-start = (bf16[48,2048]{1,0:T(8,128)(2,1)}, bf16[48,2048]{1,0:T(8,128)(2,1)S(1)}, u32[]{:S(2)}, u32[]{:S(2)}) collective-permute-start(bf16[48,2048]{1,0:T(8,128)(2,1)} %get-tuple-element.23), channel_id=1, source_target_pairs={{0,4},{4,8},{8,12},{12,16},{16,20},{20,24},{24,28},{28,32},{32,36}... | collective-permute-start | bytes 589832 | tf_op jit(solution)/shard_map/ppermute | solution.py:369
  14.4 1.3 %collective-permute-start.1 = (bf16[48,2048]{1,0:T(8,128)(2,1)}, bf16[48,2048]{1,0:T(8,128)(2,1)S(1)}, u32[]{:S(2)}, u32[]{:S(2)}) collective-permute-start(bf16[48,2048]{1,0:T(8,128)(2,1)} %get-tuple-element.24), channel_id=1, source_target_pairs={{4,0},{8,4},{12,8},{16,12},{20,16},{24,20},{28,24},{32,28},{36,32}... | collective-permute-start | bytes 589832 | tf_op jit(solution)/shard_map/ppermute | solution.py:370
  15.7 12.6 %near.2.refs_3_ = f32[32,8192]{1,0:T(8,128)} custom-call(s32[1,32]{1,0:T(1,128)} %get-tuple-element.16.refs_0_.bits, bf16[32,8192]{1,0:T(8,128)(2,1)} %get-tuple-element.17.refs_1_.dens, f32[4,8192]{1,0:T(4,128)} %get-tuple-element.18.refs_2_.geo), custom_call_target="tpu_custom_call" | custom-call | flops 6000000000 | bytes 2000000 | tf_op jit(solution)/shard_map/near/pallas_call | solution.py:374
  28.2 0.0 all-to-all-done
  28.2 0.0 copy-start
  28.2 0.6 copy-done
  28.8 2.1 %middle.1 = (bf16[16,512]{1,0:T(8,128)(2,1)}, bf16[8,16,128]{2,1,0:T(8,128)(2,1)}) custom-call(s32[1]{0:T(128)} %bitcast.4.place, bf16[256,128]{1,0:T(8,128)(2,1)} %bitcast.12, bf16[2,64,64]{2,1,0:T(8,128)(2,1)} %up.5), custom_call_target="tpu_custom_call" | custom-call | tf_op jit(solution)/shard_map/middle/pallas_call | solution.py:396
  30.9 15.6 %all-to-all-start.1 = ((bf16[8,16,128]{2,1,0:T(8,128)(2,1)}), bf16[8,16,128]{2,1,0:T(8,128)(2,1)S(1)}, u32[]{:S(2)}, u32[]{:S(2)}) async-start(bf16[8,16,128]{2,1,0:T(8,128)(2,1)} %get-tuple-element.25), calls=%async_computation.1 | async-start | bytes 65536 | tf_op jit(solution)/shard_map/all_to_all | solution.py:412
  46.5 16.9 %near.3 = f32[32,8192]{1,0:T(8,128)} custom-call(s32[1,32]{1,0:T(1,128)} %get-tuple-element.16.refs_0_.bits, bf16[32,8192]{1,0:T(8,128)(2,1)} %get-tuple-element.17.refs_1_.dens, f32[4,8192]{1,0:T(4,128)} %get-tuple-element.18.refs_2_.geo, f32[32,8192]{1,0:T(8,128)} %near.2.refs_3_, bf16[16,512]{1,0:T(8,128)(2,1)} %get-tuple-element.22.refs_4_.low_siblings), custom_call_target="tpu_custom_call" | custom-call | flops 10000000000 | bytes 2000000 | tf_op jit(solution)/shard_map/near/pallas_call | solution.py:374
  63.4 0.0 all-to-all-done.1
  63.4 0.0 copy-start.3
  63.4 0.0 collective-permute-done.below
  63.4 0.0 copy-start.1
  63.4 0.0 collective-permute-done.1.above
  63.4 0.0 copy-start.2
  63.4 0.6 copy-done.3
  64.0 0.1 copy-done.1
  64.1 0.1 copy-done.2
  64.2 15.5 %last.1 = f32[32,8192]{1,0:T(8,128)} custom-call(s32[1,32]{1,0:T(1,128)} %get-tuple-element.16.refs_0_.bits, s32[4,32]{1,0:T(4,128)} %bitcast.15, s32[1]{0:T(128)} %bitcast.4.place, f32[32,8192]{1,0:T(8,128)} %near.3, bf16[32,8192]{1,0:T(8,128)(2,1)} %get-tuple-element.17.refs_1_.dens, f32[4,8192]{1,0:T(4,128)} %get-tuple-element.18.refs_2_.geo, ...), custom_call_target="tpu_custom_call" | custom-call | tf_op jit(solution)/shard_map/last/pallas_call | solution.py:430
Async XLA Ops:
  4.8 23.4 %all-to-all-start = ((bf16[16,16,128]{2,1,0:T(8,128)(2,1)}), bf16[16,16,128]{2,1,0:T(8,128)(2,1)S(1)}, u32[]{:S(2)}, u32[]{:S(2)}) async-start(bf16[16,16,128]{2,1,0:T(8,128)(2,1)} %get-tuple-element.19), calls=%async_computation | async-start | bytes 131072 | tf_op jit(solution)/shard_map/all_to_all | solution.py:368
  12.0 51.3 %collective-permute-start = (bf16[48,2048]{1,0:T(8,128)(2,1)}, bf16[48,2048]{1,0:T(8,128)(2,1)S(1)}, u32[]{:S(2)}, u32[]{:S(2)}) collective-permute-start(bf16[48,2048]{1,0:T(8,128)(2,1)} %get-tuple-element.23), channel_id=1, source_target_pairs={{0,4},{4,8},{8,12},{12,16},{16,20},{20,24},{24,28},{28,32},{32,36}... | collective-permute-start | bytes 589832 | tf_op jit(solution)/shard_map/ppermute | solution.py:369
  14.4 49.0 %collective-permute-start.1 = (bf16[48,2048]{1,0:T(8,128)(2,1)}, bf16[48,2048]{1,0:T(8,128)(2,1)S(1)}, u32[]{:S(2)}, u32[]{:S(2)}) collective-permute-start(bf16[48,2048]{1,0:T(8,128)(2,1)} %get-tuple-element.24), channel_id=1, source_target_pairs={{4,0},{8,4},{12,8},{16,12},{20,16},{24,20},{28,24},{32,28},{36,32}... | collective-permute-start | bytes 589832 | tf_op jit(solution)/shard_map/ppermute | solution.py:370
  28.2 0.6 copy-start
  30.9 32.5 %all-to-all-start.1 = ((bf16[8,16,128]{2,1,0:T(8,128)(2,1)}), bf16[8,16,128]{2,1,0:T(8,128)(2,1)S(1)}, u32[]{:S(2)}, u32[]{:S(2)}) async-start(bf16[8,16,128]{2,1,0:T(8,128)(2,1)} %get-tuple-element.25), calls=%async_computation.1 | async-start | bytes 65536 | tf_op jit(solution)/shard_map/all_to_all | solution.py:412
  63.4 0.6 copy-start.3
  63.4 0.7 copy-start.1
  63.4 0.8 copy-start.2

commit v2 on v1

v2 whole, which is shorter than its diff:
```python
import math

import jax
import jax.numpy as jnp
from jax import lax
from jax.experimental import pallas as pl
from jax.experimental.pallas import tpu as pltpu
from jax.sharding import PartitionSpec as P

NWIN = 6
FWIN = 8
LANES = 256
F32 = jnp.float32
BF16 = jnp.bfloat16
NT = (((1,), (1,)), ((), ()))


def whole(shape):
    return pl.BlockSpec(shape, lambda *_: (0,) * len(shape))


def mm(left, right):
    return jnp.dot(left, right, preferred_element_type=F32)


def mm_nt(left, right):
    return lax.dot_general(left, right, NT, preferred_element_type=F32)


def span(cluster):
    start = cluster * LANES
    if not isinstance(start, int):
        start = pl.multiple_of(start, LANES)
    return pl.ds(start, LANES)


def pieces(value):
    high = value.astype(BF16)
    rest = value - high.astype(F32)
    middle = rest.astype(BF16)
    low = (rest - middle.astype(F32)).astype(BF16)
    return high, middle, low


def column(row):
    halves = [
        jnp.broadcast_to(row[:, at : at + 128], (128, 128)).T for at in range(0, LANES, 128)
    ]
    return jnp.concatenate(halves, axis=0)


def inverse_distance(held, spread, rows):
    parts = []
    for at in range(0, LANES, 128):
        row = rows[:, at : at + 128]
        dx = (held[0] - row[0:1]).astype(BF16)
        dy = (held[1] - row[1:2]).astype(BF16)
        dz = (held[2] - row[2:3]).astype(BF16)
        squared = (dx * dx + dy * dy) + (dz * dz + (spread[...] + row[3:4].astype(BF16)))
        parts.append(lax.rsqrt(squared))
    return jnp.concatenate(parts, axis=1)


def masked(values, bits, place):
    return values * ((bits >> place) & 1).astype(F32).astype(BF16)


def halo_message(dens_edge, geo_edge, coefs):
    edge = NWIN * LANES
    split = [piece.astype(F32) for piece in pieces(geo_edge)]
    split = jnp.concatenate(split + [jnp.zeros((4, edge), F32)], axis=0)
    wide = FWIN * 64
    coef_rows = jnp.concatenate(coefs, axis=1)
    below = jnp.concatenate([split, jnp.zeros((16, wide), F32)], axis=1).astype(BF16)
    above = jnp.concatenate([dens_edge, coef_rows], axis=1)
    return jnp.concatenate([above, below], axis=0)


def first_kernel(
    pot, geo, count, offset, basis, up, dens, scaled, coef, top, down_msg, up_msg, bits, total
):
    step = pl.program_id(0)
    steps = pl.num_programs(0)
    per_step = basis.shape[0]
    geometry = jnp.concatenate([geo[0:3, :], geo[3:4, :] * (1.0 / math.pi)], axis=0)
    scaled[...] = geometry
    coefs = []
    raised = None
    for local in range(per_step):
        rounded = pot[:, span(local)].astype(BF16)
        dens[:, span(local)] = (rounded.astype(F32) * geo[3:4, span(local)]).astype(BF16)
        value = mm_nt(rounded, basis[local]).astype(BF16)
        coef[local] = value
        coefs.append(value)
        product = mm(value, up[local])
        raised = product if raised is None else raised + product

    @pl.when(step == 0)
    def _():
        total[...] = raised
        slots = lax.broadcasted_iota(jnp.int32, offset.shape, 0)
        live = jnp.where(slots < count[...], jnp.left_shift(1, offset[...] + NWIN), 0)
        bits[...] = jnp.sum(live, axis=0, keepdims=True)
        edge = NWIN * LANES
        down_msg[...] = halo_message(dens[:, :edge], geometry[:, :edge], coefs)

    @pl.when(step > 0)
    def _():
        total[...] += raised

    @pl.when(step == steps - 1)
    def _():
        edge = (per_step - NWIN) * LANES
        up_msg[...] = halo_message(dens[:, edge:], geometry[:, edge:], coefs)
        packed = total[...]
        packed = jnp.concatenate([packed[:16], packed[16:]], axis=1).astype(BF16)
        for peer in range(top.shape[0]):
            top[peer] = packed


class Sweep:
    def __init__(self, bits, dens, geo, out, held):
        self.bits, self.dens, self.geo, self.out, self.held = bits, dens, geo, out, held
        self.clusters = dens.shape[1] // LANES
        self.turn = 0

    def prepare(self, cluster):
        held, spread = self.held[self.turn % 2]
        self.turn += 1
        rows = self.geo[:, span(cluster)]
        for k in range(3):
            held[k] = column(rows[k : k + 1])
        spread[...] = column(rows[3:4]).astype(BF16)
        return held, spread

    def run(self, cluster, ready, apart, outer):
        own = self.dens[:, span(cluster)]
        mine = self.bits[0, cluster]
        total = None
        for d in apart:
            other = cluster + d
            inside = 0 <= other < self.clusters
            if inside:
                rows, source = self.geo[:, span(other)], self.dens[:, span(other)]
            else:
                rows, source = outer(other)
            block = inverse_distance(*ready, rows)
            if d:
                source = masked(source, mine, NWIN + d)
            part = mm_nt(source, block)
            total = part if total is None else total + part
            if inside and d:
                back = masked(own, self.bits[0, other], NWIN - d)
                self.out[:, span(other)] += mm(back, block)
        self.out[:, span(cluster)] += total

    def all(self, jobs, beside=lambda index: None, outer=None):
        ready = self.prepare(jobs[0][0])
        for index, (cluster, apart) in enumerate(jobs):
            now = ready
            if index + 1 < len(jobs):
                ready = self.prepare(jobs[index + 1][0])
            self.run(cluster, now, apart, outer)
            beside(index)


def near_kernel(last, bits, dens, geo, out, held_a, held_b, spread_a, spread_b):
    out[...] = jnp.zeros_like(out)
    sweep = Sweep(bits, dens, geo, out, ((held_a, spread_a), (held_b, spread_b)))
    sweep.all([(cluster, range(NWIN + 1)) for cluster in range(last)])


def edge_kernel(
    first,
    bits,
    far,
    place,
    dens,
    geo,
    start,
    below,
    above,
    coef,
    coupling,
    down,
    sibling,
    after,
    out,
    leaf_far,
    weights_high,
    weights_low,
    held_a,
    held_b,
    spread_a,
    spread_b,
    window,
    loaded,
    arrived,
):
    clusters = coef.shape[0]
    copy = pltpu.make_async_copy(coupling, loaded, arrived)
    copy.start()
    levels = weights_high.shape[0] // 128
    edge = NWIN * LANES
    out[...] = start[...]
    weights_high[...] = jnp.zeros_like(weights_high)
    weights_low[...] = jnp.zeros_like(weights_low)

    for j in range(FWIN):
        lanes = slice(edge + j * 64, edge + (j + 1) * 64)
        window[j] = below[0:32, lanes]
        window[FWIN + clusters + j] = above[0:32, lanes]
    window[FWIN : FWIN + clusters] = coef[...]

    messages = []
    for message in (below, above):
        parts = message[32:48, :edge].astype(F32)
        messages.append((message, parts[0:4] + parts[4:8] + parts[8:12]))

    def outer(cluster):
        which, at = (0, cluster + NWIN) if cluster < 0 else (1, cluster - clusters)
        message, geometry = messages[which]
        lanes = slice(at * LANES, (at + 1) * LANES)
        return geometry[:, lanes], message[0:32, lanes]

    jobs = [(cluster, range(NWIN + 1)) for cluster in range(first, clusters)]
    jobs += [(cluster, range(-NWIN, -cluster)) for cluster in range(NWIN)]
    share = -(-clusters // (len(jobs) - 1))
    path = [None]

    def beside(index):
        if index == 0:
            copy.wait()
            return
        for cluster in range((index - 1) * share, min(clusters, index * share)):
            partners = [window[cluster + FWIN + far[m, cluster]] for m in range(4)]
            leaf_far[cluster] = mm(jnp.concatenate(partners, axis=1), loaded[cluster])
        level = index - 1
        if level < levels:
            side = (place[0] >> level) & 1
            coupled = sibling[side]
            step_down = down[side]
            if level == 0:
                weight = coupled.astype(F32)
                path[0] = step_down.astype(F32)
            else:
                high, middle, low = pieces(path[0])
                weight = mm(coupled, high) + mm(coupled, middle) + mm(coupled, low)
                path[0] = mm(step_down, high) + mm(step_down, middle) + mm(step_down, low)
            high, middle, _ = pieces(weight)
            for at in (0, 64):
                rows = slice(level * 128 + at, level * 128 + at + 64)
                weights_high[rows, at : at + 64] = high
                weights_low[rows, at : at + 64] = middle

    sweep = Sweep(bits, dens, geo, out, ((held_a, spread_a), (held_b, spread_b)))
    sweep.all(jobs, beside, outer)


def side_by_side(one):
    zero = jnp.zeros((64, 64), BF16)
    return jnp.concatenate(
        [jnp.concatenate([one, zero], axis=1), jnp.concatenate([zero, one], axis=1)], axis=0
    )


def climb(current, up, place, nodes, top):
    sides = [side_by_side(up[side]) for side in range(2)]
    levels = (current.shape[0] // 16).bit_length() - 1
    siblings = []
    base = 0
    for level in range(levels):
        count = current.shape[0] // 16
        nodes[base : base + count * 16] = current
        other = (place >> level) ^ 1
        siblings.append(nodes[pl.ds(pl.multiple_of(base + other * 16, 16), 16), :])
        base += count * 16
        if top or level + 1 < levels:
            paired = current.reshape(count // 2, 2, 16, 128)
            left = paired[:, 0].reshape(count * 8, 128)
            right = paired[:, 1].reshape(count * 8, 128)
            current = (mm(left, sides[0]) + mm(right, sides[1])).astype(BF16)
    return jnp.concatenate(siblings, axis=1), current


def middle_kernel(place, tops, up, siblings, spread, nodes):
    group = tops.shape[0] // 16
    siblings[...], root = climb(tops[...], up, place[0] & (group - 1), nodes, True)
    for peer in range(spread.shape[0]):
        spread[peer] = root


def last_kernel(
    place,
    low_siblings,
    tops,
    up,
    weights_high,
    weights_low,
    near,
    leaf_far,
    leaf_down,
    basis,
    out,
    nodes,
    local,
):
    @pl.when(pl.program_id(0) == 0)
    def _():
        below_levels = low_siblings.shape[1] // 128
        high_siblings, _ = climb(tops[...], up, place[0] >> below_levels, nodes, False)
        stacked = jnp.concatenate([low_siblings[...], high_siblings], axis=1)
        packed = mm(stacked, weights_high[...]) + mm(stacked, weights_low[...])
        value = jnp.concatenate([packed[:, :64], packed[:, 64:]], axis=0)
        local[0], local[1], _ = pieces(value)

    high, low = local[0], local[1]
    for cluster in range(basis.shape[0]):
        step_down = leaf_down[cluster]
        total = leaf_far[cluster] + (mm(high, step_down) + mm(low, step_down))
        lanes = span(cluster)
        out[:, lanes] = near[:, lanes] + mm(total.astype(BF16), basis[cluster])


def per_device(
    potential,
    geometry,
    near_count,
    near_offset,
    far_offset,
    col_basis,
    row_basis,
    leaf_up,
    leaf_down,
    leaf_coupling,
    up_transfer,
    down_transfer,
    sibling_coupling,
):
    rows, width = potential.shape
    clusters, panels, rank = col_basis.shape
    per_step = FWIN
    params = pltpu.CompilerParams(vmem_limit_bytes=56 * 2**20)
    shape = jax.ShapeDtypeStruct
    lanes = per_step * panels
    message = (48, NWIN * panels + FWIN * rank)
    devices = lax.axis_size("leaf")
    levels = devices.bit_length() - 1
    outer = 2 ** (levels // 2)
    inner = devices // outer
    dens, scaled, coef, top, down_msg, up_msg, bits = pl.pallas_call(
        first_kernel,
        grid=(clusters // per_step,),
        in_specs=[
            pl.BlockSpec((rows, lanes), lambda i: (0, i)),
            pl.BlockSpec((4, lanes), lambda i: (0, i)),
            whole((1, clusters)),
            whole((near_offset.shape[1], clusters)),
            pl.BlockSpec((per_step, rank, panels), lambda i: (i, 0, 0)),
            pl.BlockSpec((per_step, rank, rank), lambda i: (i, 0, 0)),
        ],
        out_specs=[
            pl.BlockSpec((rows, lanes), lambda i: (0, i)),
            pl.BlockSpec((4, lanes), lambda i: (0, i)),
            pl.BlockSpec((per_step, rows, rank), lambda i: (i, 0, 0)),
            whole((inner, 16, 128)),
            whole(message),
            whole(message),
            whole((1, clusters)),
        ],
        out_shape=[
            shape((rows, width), BF16),
            shape((4, width), F32),
            shape((clusters, rows, rank), BF16),
            shape((inner, 16, 128), BF16),
            shape(message, BF16),
            shape(message, BF16),
            shape((1, clusters), jnp.int32),
        ],
        scratch_shapes=[pltpu.VMEM((rows, rank), F32)],
        compiler_params=params,
        name="first",
    )(
        potential,
        geometry,
        near_count.reshape(1, clusters),
        near_offset.T,
        col_basis.transpose(0, 2, 1),
        leaf_up,
    )
    upward = [(i, i + 1) for i in range(devices - 1)]
    downward = [(j, i) for i, j in upward]
    near_groups = [[at * inner + i for i in range(inner)] for at in range(outer)]
    far_groups = [[at * inner + i for at in range(outer)] for i in range(inner)]
    place = lax.axis_index("leaf").reshape(1).astype(jnp.int32)
    tops = lax.all_to_all(top, "leaf", 0, 0, axis_index_groups=near_groups)
    below = lax.ppermute(up_msg, "leaf", upward)
    above = lax.ppermute(down_msg, "leaf", downward)

    columns = [pltpu.VMEM((3, panels, 128), F32)] * 2 + [pltpu.VMEM((panels, 128), BF16)] * 2
    cut = 12
    near = pl.pallas_call(
        lambda *refs: near_kernel(cut, *refs),
        grid_spec=pltpu.PrefetchScalarGridSpec(
            num_scalar_prefetch=1,
            grid=(1,),
            in_specs=[whole((rows, width)), whole((4, width))],
            out_specs=whole((rows, width)),
            scratch_shapes=columns,
        ),
        out_shape=shape((rows, width), F32),
        compiler_params=params,
        cost_estimate=pl.CostEstimate(
            flops=6 * 10**9, transcendentals=84 * 65536, bytes_accessed=2 * 10**6
        ),
        name="near",
    )(bits, dens, scaled)
    tops, near = lax.optimization_barrier((tops, near))
    low_siblings, spread = pl.pallas_call(
        middle_kernel,
        grid_spec=pltpu.PrefetchScalarGridSpec(
            num_scalar_prefetch=1,
            grid=(1,),
            in_specs=[whole((inner * 16, 128)), whole(up_transfer.shape)],
            out_specs=[whole((16, (inner.bit_length() - 1) * 128)), whole((outer, 16, 128))],
            scratch_shapes=[pltpu.VMEM((inner * 32, 128), BF16)],
        ),
        out_shape=[
            shape((16, (inner.bit_length() - 1) * 128), BF16),
            shape((outer, 16, 128), BF16),
        ],
        compiler_params=params,
        name="middle",
    )(place, tops.reshape(inner * 16, 128), up_transfer)
    tops = lax.all_to_all(spread, "leaf", 0, 0, axis_index_groups=far_groups)
    operands = (
        dens,
        scaled,
        near,
        below,
        above,
        coef,
        leaf_coupling.reshape(clusters, 4 * rank, rank),
        down_transfer,
        sibling_coupling,
        low_siblings,
    )
    specs = [whole(x.shape) for x in operands]
    specs[6] = pl.BlockSpec(memory_space=pl.ANY)
    weights = (levels * 128, 128)
    near, leaf_far, weights_high, weights_low = pl.pallas_call(
        lambda *refs: edge_kernel(cut, *refs),
        grid_spec=pltpu.PrefetchScalarGridSpec(
            num_scalar_prefetch=3,
            grid=(1,),
            in_specs=specs,
            out_specs=[
                whole((rows, width)),
                whole((clusters, rows, rank)),
                whole(weights),
                whole(weights),
            ],
            scratch_shapes=columns
            + [
                pltpu.VMEM((clusters + 2 * FWIN, rows, rank), BF16),
                pltpu.VMEM((clusters, 4 * rank, rank), BF16),
                pltpu.SemaphoreType.DMA,
            ],
        ),
        out_shape=[
            shape((rows, width), F32),
            shape((clusters, rows, rank), F32),
            shape(weights, BF16),
            shape(weights, BF16),
        ],
        compiler_params=params,
        cost_estimate=pl.CostEstimate(
            flops=12 * 10**9, transcendentals=161 * 65536, bytes_accessed=4 * 10**6
        ),
        name="edge",
    )(bits, far_offset.T, place, *operands)

    def chunk(tail):
        return pl.BlockSpec((per_step,) + tail, lambda i, *_: (i,) + (0,) * len(tail))

    strip = pl.BlockSpec((rows, lanes), lambda i, *_: (0, i))
    return pl.pallas_call(
        last_kernel,
        grid_spec=pltpu.PrefetchScalarGridSpec(
            num_scalar_prefetch=1,
            grid=(clusters // per_step,),
            in_specs=[
                whole(low_siblings.shape),
                whole((outer * 16, 128)),
                whole(up_transfer.shape),
                whole(weights),
                whole(weights),
                strip,
                chunk((rows, rank)),
                chunk((rank, rank)),
                chunk((rank, panels)),
            ],
            out_specs=strip,
            scratch_shapes=[
                pltpu.VMEM((outer * 32, 128), BF16),
                pltpu.VMEM((2, rows, rank), BF16),
            ],
        ),
        out_shape=shape((rows, width), F32),
        compiler_params=params,
        name="last",
    )(
        place,
        low_siblings,
        tops.reshape(outer * 16, 128),
        up_transfer,
        weights_high,
        weights_low,
        near,
        leaf_far,
        leaf_down,
        row_basis.transpose(0, 2, 1),
    )


def solution(mesh):
    placed = (
        P("rhs", "leaf"),
        P(None, "leaf"),
        P("leaf"),
        P("leaf", None),
        P("leaf", None),
        P("leaf", None, None),
        P("leaf", None, None),
        P("leaf", None, None),
        P("leaf", None, None),
        P("leaf", None, None, None),
        P(),
        P(),
        P(),
    )
    return jax.shard_map(
        per_device, mesh=mesh, in_specs=placed, out_specs=P("rhs", "leaf"), check_vma=False
    )
```

time: 80.1 us -> 73.9 us (0.923)
  Pallas kernels: 51.8 us -> 44.9 us
    pallas_call x1, Pallas kernels: 15.5 us -> 7.47 us  [per_device(): pl.pallas_call(last_kernel, grid_spec=pltpu.PrefetchScalarGridSpec(num_sc...]
    pallas_call x2, Pallas kernels: 29.5 us -> 30.5 us  [the longest x1 20 us: per_device(): pl.pallas_call(lambda *refs: edge_kernel(cut, *refs), grid_spec=pltpu.Pre...]
  transfers between devices with their start and end apart: 4 -> 4, of which waited for: 0 -> 0; matrix products, arithmetic and copies ran while one was open for 0% -> 0% of each run, Pallas kernels for 40% -> 44%
where the time goes in v2:
time: 73.9 us; the launch traced here: 73.3 us
  Pallas kernels  44.9 us (61%)
  starting transfers between devices  26.4 us (36%)
  local copies, waits for them, and re-layouts  1.98 us (3%)
    pallas_call x1, Pallas kernels, per_device(): pl.pallas_call(lambda *refs: edge_kernel(cut, *refs), grid_spec=pltpu.Pre...  20 us
    all_to_all x1, starting transfers between devices, per_device(): tops = lax.all_to_all(spread, 'leaf', 0, 0, axis_index_groups=far_groups)  15.6 us
    pallas_call x1, Pallas kernels, per_device(): pl.pallas_call(lambda *refs: near_kernel(cut, *refs), grid_spec=pltpu.Pre...  10.5 us
    pallas_call x1, Pallas kernels, per_device(): pl.pallas_call(last_kernel, grid_spec=pltpu.PrefetchScalarGridSpec(num_sc...  7.47 us
    all_to_all x1, starting transfers between devices, per_device(): tops = lax.all_to_all(top, 'leaf', 0, 0, axis_index_groups=near_groups)  7.22 us
    pallas_call x1, Pallas kernels, per_device(): pl.pallas_call(first_kernel, grid=(clusters // per_step,), in_specs=[pl.B...  4.84 us
    ppermute x1, starting transfers between devices, per_device(): below = lax.ppermute(up_msg, 'leaf', upward)  2.31 us
    pallas_call x1, Pallas kernels, per_device(): pl.pallas_call(middle_kernel, grid_spec=pltpu.PrefetchScalarGridSpec(num_...  2.08 us
  transfers between devices with their start and end apart: 4, of which 0 were waited for; matrix products, arithmetic and copies ran while one was open for 0% of the time, Pallas kernels for 44%

profile of v2, /device:TPU:6, one launch (start us, length us, event | category | flops | bytes accessed | tf_op | source)
XLA Modules:
  0.0 73.3 jit_solution(2905655148285161144)
XLA Ops:
  0.0 4.8 %first.1 = (bf16[32,8192]{1,0:T(8,128)(2,1)}, f32[4,8192]{1,0:T(4,128)}, bf16[32,32,64]{2,1,0:T(8,128)(2,1)}, bf16[16,16,128]{2,1,0:T(8,128)(2,1)}, bf16[48,2048...) custom-call(f32[32,8192]{1,0:T(8,128)} %pot.1, f32[4,8192]{1,0:T(4,128)} %geo.1, s32[1,32]{1,0:T(1,128)} %bitcast.14, ...), custom_call_target="tpu_custom_call" | custom-call | tf_op jit(solution)/shard_map/first/pallas_call | solution.py:351
  4.8 7.2 %all-to-all-start = ((bf16[16,16,128]{2,1,0:T(8,128)(2,1)}), bf16[16,16,128]{2,1,0:T(8,128)(2,1)S(1)}, u32[]{:S(2)}, u32[]{:S(2)}) async-start(bf16[16,16,128]{2,1,0:T(8,128)(2,1)} %get-tuple-element.20), calls=%async_computation | async-start | bytes 131072 | tf_op jit(solution)/shard_map/all_to_all | solution.py:396
  12.1 2.3 %collective-permute-start = (bf16[48,2048]{1,0:T(8,128)(2,1)}, bf16[48,2048]{1,0:T(8,128)(2,1)S(1)}, u32[]{:S(2)}, u32[]{:S(2)}) collective-permute-start(bf16[48,2048]{1,0:T(8,128)(2,1)} %get-tuple-element.28), channel_id=1, source_target_pairs={{0,4},{4,8},{8,12},{12,16},{16,20},{20,24},{24,28},{28,32},{32,36}... | collective-permute-start | bytes 589832 | tf_op jit(solution)/shard_map/ppermute | solution.py:397
  14.4 1.3 %collective-permute-start.1 = (bf16[48,2048]{1,0:T(8,128)(2,1)}, bf16[48,2048]{1,0:T(8,128)(2,1)S(1)}, u32[]{:S(2)}, u32[]{:S(2)}) collective-permute-start(bf16[48,2048]{1,0:T(8,128)(2,1)} %get-tuple-element.29), channel_id=1, source_target_pairs={{4,0},{8,4},{12,8},{16,12},{20,16},{24,20},{28,24},{32,28},{36,32}... | collective-permute-start | bytes 589832 | tf_op jit(solution)/shard_map/ppermute | solution.py:398
  15.7 10.5 %near.1.refs_5_ = f32[32,8192]{1,0:T(8,128)} custom-call(s32[1,32]{1,0:T(1,128)} %get-tuple-element.21.refs_0_, bf16[32,8192]{1,0:T(8,128)(2,1)} %get-tuple-element.22.refs_1_.refs_3_, f32[4,8192]{1,0:T(4,128)} %get-tuple-element.23.refs_2_.refs_4_), custom_call_target="tpu_custom_call" | custom-call | flops 6000000000 | bytes 2000000 | tf_op jit(solution)/shard_map/near/pallas_call | solution.py:402
  26.2 0.0 all-to-all-done
  26.2 0.0 copy-start
  26.2 0.6 copy-done
  26.8 2.1 %middle.1 = (bf16[16,512]{1,0:T(8,128)(2,1)}, bf16[8,16,128]{2,1,0:T(8,128)(2,1)}) custom-call(s32[1]{0:T(128)} %bitcast.place.refs_2_, bf16[256,128]{1,0:T(8,128)(2,1)} %bitcast.11, bf16[2,64,64]{2,1,0:T(8,128)(2,1)} %up.5), custom_call_target="tpu_custom_call" | custom-call | tf_op jit(solution)/shard_map/middle/pallas_call | solution.py:419
  28.9 15.6 %all-to-all-start.1 = ((bf16[8,16,128]{2,1,0:T(8,128)(2,1)}), bf16[8,16,128]{2,1,0:T(8,128)(2,1)S(1)}, u32[]{:S(2)}, u32[]{:S(2)}) async-start(bf16[8,16,128]{2,1,0:T(8,128)(2,1)} %get-tuple-element.26), calls=%async_computation.1 | async-start | bytes 65536 | tf_op jit(solution)/shard_map/all_to_all | solution.py:435
  44.5 0.0 collective-permute-done.refs_6_
  44.5 0.0 copy-start.2
  44.5 0.0 collective-permute-done.1.refs_7_
  44.5 0.0 copy-start.3
  44.5 0.7 copy-done.2
  45.2 0.1 copy-done.3
  45.2 20.0 %edge.1 = (f32[32,8192]{1,0:T(8,128)}, f32[32,32,64]{2,1,0:T(8,128)}, bf16[896,128]{1,0:T(8,128)(2,1)}, bf16[896,128]{1,0:T(8,128)(2,1)}) custom-call(s32[1,32]{1,0:T(1,128)} %get-tuple-element.21.refs_0_, s32[4,32]{1,0:T(4,128)} %bitcast.16, s32[1]{0:T(128)} %bitcast.place.refs_2_, bf16[32,8192]{1,0:T(8,128)(2,1)} %get-tuple-element.22.refs_1_.refs_3_, ...), custom_call_target="tpu_custom_call" | custom-call | flops 12000000000 | bytes 4000000 | tf_op jit(solution)/shard_map/edge/pallas_call | solution.py:451
  65.2 0.0 all-to-all-done.1
  65.2 0.0 copy-start.1
  65.2 0.6 copy-done.1
  65.9 7.5 %last.1 = f32[32,8192]{1,0:T(8,128)} custom-call(s32[1]{0:T(128)} %bitcast.place.refs_2_, bf16[16,512]{1,0:T(8,128)(2,1)} %get-tuple-element.25.refs_12_.low_siblings, bf16[128,128]{1,0:T(8,128)(2,1)} %bitcast.12, bf16[2,64,64]{2,1,0:T(8,128)(2,1)} %up.5, bf16[896,128]{1,0:T(8,128)(2,1)} %get-tuple-element.31.weights_high, ...), custom_call_target="tpu_custom_call" | custom-call | tf_op jit(solution)/shard_map/last/pallas_call | solution.py:487
Async XLA Ops:
  4.8 21.3 %all-to-all-start = ((bf16[16,16,128]{2,1,0:T(8,128)(2,1)}), bf16[16,16,128]{2,1,0:T(8,128)(2,1)S(1)}, u32[]{:S(2)}, u32[]{:S(2)}) async-start(bf16[16,16,128]{2,1,0:T(8,128)(2,1)} %get-tuple-element.20), calls=%async_computation | async-start | bytes 131072 | tf_op jit(solution)/shard_map/all_to_all | solution.py:396
  12.1 32.4 %collective-permute-start = (bf16[48,2048]{1,0:T(8,128)(2,1)}, bf16[48,2048]{1,0:T(8,128)(2,1)S(1)}, u32[]{:S(2)}, u32[]{:S(2)}) collective-permute-start(bf16[48,2048]{1,0:T(8,128)(2,1)} %get-tuple-element.28), channel_id=1, source_target_pairs={{0,4},{4,8},{8,12},{12,16},{16,20},{20,24},{24,28},{28,32},{32,36}... | collective-permute-start | bytes 589832 | tf_op jit(solution)/shard_map/ppermute | solution.py:397
  14.4 30.1 %collective-permute-start.1 = (bf16[48,2048]{1,0:T(8,128)(2,1)}, bf16[48,2048]{1,0:T(8,128)(2,1)S(1)}, u32[]{:S(2)}, u32[]{:S(2)}) collective-permute-start(bf16[48,2048]{1,0:T(8,128)(2,1)} %get-tuple-element.29), channel_id=1, source_target_pairs={{4,0},{8,4},{12,8},{16,12},{20,16},{24,20},{28,24},{32,28},{36,32}... | collective-permute-start | bytes 589832 | tf_op jit(solution)/shard_map/ppermute | solution.py:398
  26.2 0.6 copy-start
  28.9 36.3 %all-to-all-start.1 = ((bf16[8,16,128]{2,1,0:T(8,128)(2,1)}), bf16[8,16,128]{2,1,0:T(8,128)(2,1)S(1)}, u32[]{:S(2)}, u32[]{:S(2)}) async-start(bf16[8,16,128]{2,1,0:T(8,128)(2,1)} %get-tuple-element.26), calls=%async_computation.1 | async-start | bytes 65536 | tf_op jit(solution)/shard_map/all_to_all | solution.py:435
  44.5 0.7 copy-start.2
  44.5 0.8 %copy-start.3 = (bf16[48,2048]{1,0:T(8,128)(2,1)}, bf16[48,2048]{1,0:T(8,128)(2,1)S(1)}, u32[]{:S(2)}) copy-start(bf16[48,2048]{1,0:T(8,128)(2,1)S(1)} %collective-permute-done.1.refs_7_) | copy-start | bytes 589828
  65.2 0.6 copy-start.1

commit v3 on v2

--- a/solution.py
+++ b/solution.py
@@ -13,6 +13,10 @@
 F32 = jnp.float32
 BF16 = jnp.bfloat16
 NT = (((1,), (1,)), ((), ()))
+
+
+def keep(value):
+    return pltpu.with_memory_space_constraint(value, pltpu.VMEM)
 
 
 def whole(shape):
@@ -420,8 +424,7 @@
         middle_kernel,
         grid_spec=pltpu.PrefetchScalarGridSpec(
             num_scalar_prefetch=1,
-            grid=(1,),
-            in_specs=[whole((inner * 16, 128)), whole(up_transfer.shape)],
+            in_specs=[pl.BlockSpec(memory_space=pltpu.VMEM), whole(up_transfer.shape)],
             out_specs=[whole((16, (inner.bit_length() - 1) * 128)), whole((outer, 16, 128))],
             scratch_shapes=[pltpu.VMEM((inner * 32, 128), BF16)],
         ),
@@ -431,14 +434,14 @@
         ],
         compiler_params=params,
         name="middle",
-    )(place, tops.reshape(inner * 16, 128), up_transfer)
+    )(place, keep(tops.reshape(inner * 16, 128)), up_transfer)
     tops = lax.all_to_all(spread, "leaf", 0, 0, axis_index_groups=far_groups)
     operands = (
         dens,
         scaled,
         near,
-        below,
-        above,
+        keep(below),
+        keep(above),
         coef,
         leaf_coupling.reshape(clusters, 4 * rank, rank),
         down_transfer,
@@ -447,6 +450,7 @@
     )
     specs = [whole(x.shape) for x in operands]
     specs[6] = pl.BlockSpec(memory_space=pl.ANY)
+    specs[3] = specs[4] = pl.BlockSpec(memory_space=pltpu.VMEM)
     weights = (levels * 128, 128)
     near, leaf_far, weights_high, weights_low = pl.pallas_call(
         lambda *refs: edge_kernel(cut, *refs),
@@ -491,7 +495,7 @@
             grid=(clusters // per_step,),
             in_specs=[
                 whole(low_siblings.shape),
-                whole((outer * 16, 128)),
+                pl.BlockSpec(memory_space=pltpu.VMEM),
                 whole(up_transfer.shape),
                 whole(weights),
                 whole(weights),
@@ -512,7 +516,7 @@
     )(
         place,
         low_siblings,
-        tops.reshape(outer * 16, 128),
+        keep(tops.reshape(outer * 16, 128)),
         up_transfer,
         weights_high,
         weights_low,

time: 73.9 us -> 72.1 us (0.976)
  local copies, waits for them, and re-layouts: 1.98 us -> 0 us
    unnamed x8 -> x0, local copies, waits for them, and re-layouts: 1.98 us -> none
  transfers between devices with their start and end apart: 4 -> 4, of which waited for: 0 -> 0; matrix products, arithmetic and copies ran while one was open for 0% -> 0% of each run, Pallas kernels for 44% -> 46%
where the time goes in v3:
time: 72.1 us; the launch traced here: 71.5 us
  Pallas kernels  45 us (62%)
  starting transfers between devices  26.4 us (37%)
    pallas_call x1, Pallas kernels, per_device(): pl.pallas_call(lambda *refs: edge_kernel(cut, *refs), grid_spec=pltpu.Pre...  20.2 us
    all_to_all x1, starting transfers between devices, per_device(): tops = lax.all_to_all(spread, 'leaf', 0, 0, axis_index_groups=far_groups)  15.6 us
    pallas_call x1, Pallas kernels, per_device(): pl.pallas_call(lambda *refs: near_kernel(cut, *refs), grid_spec=pltpu.Pre...  10.5 us
    pallas_call x1, Pallas kernels, per_device(): pl.pallas_call(last_kernel, grid_spec=pltpu.PrefetchScalarGridSpec(num_sc...  7.51 us
    all_to_all x1, starting transfers between devices, per_device(): tops = lax.all_to_all(top, 'leaf', 0, 0, axis_index_groups=near_groups)  7.22 us
    pallas_call x1, Pallas kernels, per_device(): pl.pallas_call(first_kernel, grid=(clusters // per_step,), in_specs=[pl.B...  4.8 us
    ppermute x1, starting transfers between devices, per_device(): below = lax.ppermute(up_msg, 'leaf', upward)  2.31 us
    pallas_call x1, Pallas kernels, per_device(): pl.pallas_call(middle_kernel, grid_spec=pltpu.PrefetchScalarGridSpec(num_...  1.98 us
  transfers between devices with their start and end apart: 4, of which 0 were waited for; matrix products, arithmetic and copies ran while one was open for 0% of the time, Pallas kernels for 46%

profile of v3, /device:TPU:6, one launch (start us, length us, event | category | flops | bytes accessed | tf_op | source)
XLA Modules:
  0.0 71.5 jit_solution(5967522521007541351)
XLA Ops:
  0.0 4.8 %first.1 = (bf16[32,8192]{1,0:T(8,128)(2,1)}, f32[4,8192]{1,0:T(4,128)}, bf16[32,32,64]{2,1,0:T(8,128)(2,1)}, bf16[16,16,128]{2,1,0:T(8,128)(2,1)}, bf16[48,2048...) custom-call(f32[32,8192]{1,0:T(8,128)} %pot.1, f32[4,8192]{1,0:T(4,128)} %geo.1, s32[1,32]{1,0:T(1,128)} %bitcast.14, ...), custom_call_target="tpu_custom_call" | custom-call | tf_op jit(solution)/shard_map/first/pallas_call | solution.py:355
  4.8 7.2 %all-to-all-start = ((bf16[16,16,128]{2,1,0:T(8,128)(2,1)}), bf16[16,16,128]{2,1,0:T(8,128)(2,1)S(1)}, u32[]{:S(2)}, u32[]{:S(2)}) async-start(bf16[16,16,128]{2,1,0:T(8,128)(2,1)} %get-tuple-element.20), calls=%async_computation | async-start | bytes 131072 | tf_op jit(solution)/shard_map/all_to_all | solution.py:400
  12.0 2.3 %collective-permute-start = (bf16[48,2048]{1,0:T(8,128)(2,1)}, bf16[48,2048]{1,0:T(8,128)(2,1)S(1)}, u32[]{:S(2)}, u32[]{:S(2)}) collective-permute-start(bf16[48,2048]{1,0:T(8,128)(2,1)} %get-tuple-element.28), channel_id=1, source_target_pairs={{0,4},{4,8},{8,12},{12,16},{16,20},{20,24},{24,28},{28,32},{32,36}... | collective-permute-start | bytes 589832 | tf_op jit(solution)/shard_map/ppermute | solution.py:401
  14.4 1.3 %collective-permute-start.1 = (bf16[48,2048]{1,0:T(8,128)(2,1)}, bf16[48,2048]{1,0:T(8,128)(2,1)S(1)}, u32[]{:S(2)}, u32[]{:S(2)}) collective-permute-start(bf16[48,2048]{1,0:T(8,128)(2,1)} %get-tuple-element.29), channel_id=1, source_target_pairs={{4,0},{8,4},{12,8},{16,12},{20,16},{24,20},{28,24},{32,28},{36,32}... | collective-permute-start | bytes 589832 | tf_op jit(solution)/shard_map/ppermute | solution.py:402
  15.7 10.5 %near.1.refs_5_ = f32[32,8192]{1,0:T(8,128)} custom-call(s32[1,32]{1,0:T(1,128)} %get-tuple-element.21.refs_0_, bf16[32,8192]{1,0:T(8,128)(2,1)} %get-tuple-element.22.refs_1_.refs_3_, f32[4,8192]{1,0:T(4,128)} %get-tuple-element.23.refs_2_.refs_4_), custom_call_target="tpu_custom_call" | custom-call | flops 6000000000 | bytes 2000000 | tf_op jit(solution)/shard_map/near/pallas_call | solution.py:406
  26.1 0.0 all-to-all-done
  26.1 2.0 %middle.1 = (bf16[16,512]{1,0:T(8,128)(2,1)}, bf16[8,16,128]{2,1,0:T(8,128)(2,1)}) custom-call(s32[1]{0:T(128)} %bitcast.place.refs_2_, bf16[256,128]{1,0:T(8,128)(2,1)S(1)} %bitcast.9, bf16[2,64,64]{2,1,0:T(8,128)(2,1)} %up.5), custom_call_target="tpu_custom_call" | custom-call | tf_op jit(solution)/shard_map/middle/pallas_call | solution.py:423
  28.1 15.6 %all-to-all-start.1 = ((bf16[8,16,128]{2,1,0:T(8,128)(2,1)}), bf16[8,16,128]{2,1,0:T(8,128)(2,1)S(1)}, u32[]{:S(2)}, u32[]{:S(2)}) async-start(bf16[8,16,128]{2,1,0:T(8,128)(2,1)} %get-tuple-element.26), calls=%async_computation.1 | async-start | bytes 65536 | tf_op jit(solution)/shard_map/all_to_all | solution.py:438
  43.7 0.0 collective-permute-done.refs_6_
  43.7 0.0 collective-permute-done.1.refs_7_
  43.7 20.2 %edge.1 = (f32[32,8192]{1,0:T(8,128)}, f32[32,32,64]{2,1,0:T(8,128)}, bf16[896,128]{1,0:T(8,128)(2,1)}, bf16[896,128]{1,0:T(8,128)(2,1)}) custom-call(s32[1,32]{1,0:T(1,128)} %get-tuple-element.21.refs_0_, s32[4,32]{1,0:T(4,128)} %bitcast.16, s32[1]{0:T(128)} %bitcast.place.refs_2_, bf16[32,8192]{1,0:T(8,128)(2,1)} %get-tuple-element.22.refs_1_.refs_3_, ...), custom_call_target="tpu_custom_call" | custom-call | flops 12000000000 | bytes 4000000 | tf_op jit(solution)/shard_map/edge/pallas_call | solution.py:455
  63.9 0.0 all-to-all-done.1
  63.9 7.5 %last.1 = f32[32,8192]{1,0:T(8,128)} custom-call(s32[1]{0:T(128)} %bitcast.place.refs_2_, bf16[16,512]{1,0:T(8,128)(2,1)} %get-tuple-element.25.refs_12_.low_siblings, bf16[128,128]{1,0:T(8,128)(2,1)S(1)} %bitcast.10, bf16[2,64,64]{2,1,0:T(8,128)(2,1)} %up.5, bf16[896,128]{1,0:T(8,128)(2,1)} %get-tuple-element.31.weights_high, ...), custom_call_target="tpu_custom_call" | custom-call | tf_op jit(solution)/shard_map/last/pallas_call | solution.py:491
Async XLA Ops:
  4.8 21.3 %all-to-all-start = ((bf16[16,16,128]{2,1,0:T(8,128)(2,1)}), bf16[16,16,128]{2,1,0:T(8,128)(2,1)S(1)}, u32[]{:S(2)}, u32[]{:S(2)}) async-start(bf16[16,16,128]{2,1,0:T(8,128)(2,1)} %get-tuple-element.20), calls=%async_computation | async-start | bytes 131072 | tf_op jit(solution)/shard_map/all_to_all | solution.py:400
  12.0 31.7 %collective-permute-start = (bf16[48,2048]{1,0:T(8,128)(2,1)}, bf16[48,2048]{1,0:T(8,128)(2,1)S(1)}, u32[]{:S(2)}, u32[]{:S(2)}) collective-permute-start(bf16[48,2048]{1,0:T(8,128)(2,1)} %get-tuple-element.28), channel_id=1, source_target_pairs={{0,4},{4,8},{8,12},{12,16},{16,20},{20,24},{24,28},{28,32},{32,36}... | collective-permute-start | bytes 589832 | tf_op jit(solution)/shard_map/ppermute | solution.py:401
  14.4 29.3 %collective-permute-start.1 = (bf16[48,2048]{1,0:T(8,128)(2,1)}, bf16[48,2048]{1,0:T(8,128)(2,1)S(1)}, u32[]{:S(2)}, u32[]{:S(2)}) collective-permute-start(bf16[48,2048]{1,0:T(8,128)(2,1)} %get-tuple-element.29), channel_id=1, source_target_pairs={{4,0},{8,4},{12,8},{16,12},{20,16},{24,20},{28,24},{32,28},{36,32}... | collective-permute-start | bytes 589832 | tf_op jit(solution)/shard_map/ppermute | solution.py:402
  28.1 35.8 %all-to-all-start.1 = ((bf16[8,16,128]{2,1,0:T(8,128)(2,1)}), bf16[8,16,128]{2,1,0:T(8,128)(2,1)S(1)}, u32[]{:S(2)}, u32[]{:S(2)}) async-start(bf16[8,16,128]{2,1,0:T(8,128)(2,1)} %get-tuple-element.26), calls=%async_computation.1 | async-start | bytes 65536 | tf_op jit(solution)/shard_map/all_to_all | solution.py:438

commit v4 on v3

--- a/solution.py
+++ b/solution.py
@@ -485,14 +485,14 @@
     )(bits, far_offset.T, place, *operands)
 
     def chunk(tail):
-        return pl.BlockSpec((per_step,) + tail, lambda i, *_: (i,) + (0,) * len(tail))
-
-    strip = pl.BlockSpec((rows, lanes), lambda i, *_: (0, i))
+        return pl.BlockSpec((2 * per_step,) + tail, lambda i, *_: (i,) + (0,) * len(tail))
+
+    strip = pl.BlockSpec((rows, 2 * lanes), lambda i, *_: (0, i))
     return pl.pallas_call(
         last_kernel,
         grid_spec=pltpu.PrefetchScalarGridSpec(
             num_scalar_prefetch=1,
-            grid=(clusters // per_step,),
+            grid=(clusters // (2 * per_step),),
             in_specs=[
                 whole(low_siblings.shape),
                 pl.BlockSpec(memory_space=pltpu.VMEM),

time: 72.1 us -> 72 us (level)
  no operation moved by 1% of the time
where the time goes in v4:
time: 72 us; the launch traced here: 71.5 us
  Pallas kernels  45 us (62%)
  starting transfers between devices  26.4 us (37%)
    pallas_call x1, Pallas kernels, per_device(): pl.pallas_call(lambda *refs: edge_kernel(cut, *refs), grid_spec=pltpu.Pre...  20.2 us
    all_to_all x1, starting transfers between devices, per_device(): tops = lax.all_to_all(spread, 'leaf', 0, 0, axis_index_groups=far_groups)  15.6 us
    pallas_call x1, Pallas kernels, per_device(): pl.pallas_call(lambda *refs: near_kernel(cut, *refs), grid_spec=pltpu.Pre...  10.5 us
    pallas_call x1, Pallas kernels, per_device(): pl.pallas_call(last_kernel, grid_spec=pltpu.PrefetchScalarGridSpec(num_sc...  7.53 us
    all_to_all x1, starting transfers between devices, per_device(): tops = lax.all_to_all(top, 'leaf', 0, 0, axis_index_groups=near_groups)  7.22 us
    pallas_call x1, Pallas kernels, per_device(): pl.pallas_call(first_kernel, grid=(clusters // per_step,), in_specs=[pl.B...  4.8 us
    ppermute x1, starting transfers between devices, per_device(): below = lax.ppermute(up_msg, 'leaf', upward)  2.31 us
    pallas_call x1, Pallas kernels, per_device(): pl.pallas_call(middle_kernel, grid_spec=pltpu.PrefetchScalarGridSpec(num_...  1.98 us
  transfers between devices with their start and end apart: 4, of which 0 were waited for; matrix products, arithmetic and copies ran while one was open for 0% of the time, Pallas kernels for 46%

profile of v4, /device:TPU:6, one launch (start us, length us, event | category | flops | bytes accessed | tf_op | source)
XLA Modules:
  0.0 71.5 jit_solution(6328161182049137141)
XLA Ops:
  0.0 4.8 %first.1 = (bf16[32,8192]{1,0:T(8,128)(2,1)}, f32[4,8192]{1,0:T(4,128)}, bf16[32,32,64]{2,1,0:T(8,128)(2,1)}, bf16[16,16,128]{2,1,0:T(8,128)(2,1)}, bf16[48,2048...) custom-call(f32[32,8192]{1,0:T(8,128)} %pot.1, f32[4,8192]{1,0:T(4,128)} %geo.1, s32[1,32]{1,0:T(1,128)} %bitcast.14, ...), custom_call_target="tpu_custom_call" | custom-call | tf_op jit(solution)/shard_map/first/pallas_call | solution.py:355
  4.8 7.2 %all-to-all-start = ((bf16[16,16,128]{2,1,0:T(8,128)(2,1)}), bf16[16,16,128]{2,1,0:T(8,128)(2,1)S(1)}, u32[]{:S(2)}, u32[]{:S(2)}) async-start(bf16[16,16,128]{2,1,0:T(8,128)(2,1)} %get-tuple-element.20), calls=%async_computation | async-start | bytes 131072 | tf_op jit(solution)/shard_map/all_to_all | solution.py:400
  12.0 2.3 %collective-permute-start = (bf16[48,2048]{1,0:T(8,128)(2,1)}, bf16[48,2048]{1,0:T(8,128)(2,1)S(1)}, u32[]{:S(2)}, u32[]{:S(2)}) collective-permute-start(bf16[48,2048]{1,0:T(8,128)(2,1)} %get-tuple-element.28), channel_id=1, source_target_pairs={{0,4},{4,8},{8,12},{12,16},{16,20},{20,24},{24,28},{28,32},{32,36}... | collective-permute-start | bytes 589832 | tf_op jit(solution)/shard_map/ppermute | solution.py:401
  14.4 1.3 %collective-permute-start.1 = (bf16[48,2048]{1,0:T(8,128)(2,1)}, bf16[48,2048]{1,0:T(8,128)(2,1)S(1)}, u32[]{:S(2)}, u32[]{:S(2)}) collective-permute-start(bf16[48,2048]{1,0:T(8,128)(2,1)} %get-tuple-element.29), channel_id=1, source_target_pairs={{4,0},{8,4},{12,8},{16,12},{20,16},{24,20},{28,24},{32,28},{36,32}... | collective-permute-start | bytes 589832 | tf_op jit(solution)/shard_map/ppermute | solution.py:402
  15.7 10.5 %near.1.refs_5_ = f32[32,8192]{1,0:T(8,128)} custom-call(s32[1,32]{1,0:T(1,128)} %get-tuple-element.21.refs_0_, bf16[32,8192]{1,0:T(8,128)(2,1)} %get-tuple-element.22.refs_1_.refs_3_, f32[4,8192]{1,0:T(4,128)} %get-tuple-element.23.refs_2_.refs_4_), custom_call_target="tpu_custom_call" | custom-call | flops 6000000000 | bytes 2000000 | tf_op jit(solution)/shard_map/near/pallas_call | solution.py:406
  26.1 0.0 all-to-all-done
  26.1 2.0 %middle.1 = (bf16[16,512]{1,0:T(8,128)(2,1)}, bf16[8,16,128]{2,1,0:T(8,128)(2,1)}) custom-call(s32[1]{0:T(128)} %bitcast.place.refs_2_, bf16[256,128]{1,0:T(8,128)(2,1)S(1)} %bitcast.9, bf16[2,64,64]{2,1,0:T(8,128)(2,1)} %up.5), custom_call_target="tpu_custom_call" | custom-call | tf_op jit(solution)/shard_map/middle/pallas_call | solution.py:423
  28.1 15.6 %all-to-all-start.1 = ((bf16[8,16,128]{2,1,0:T(8,128)(2,1)}), bf16[8,16,128]{2,1,0:T(8,128)(2,1)S(1)}, u32[]{:S(2)}, u32[]{:S(2)}) async-start(bf16[8,16,128]{2,1,0:T(8,128)(2,1)} %get-tuple-element.26), calls=%async_computation.1 | async-start | bytes 65536 | tf_op jit(solution)/shard_map/all_to_all | solution.py:438
  43.7 0.0 collective-permute-done.refs_6_
  43.7 0.0 collective-permute-done.1.refs_7_
  43.7 20.2 %edge.1 = (f32[32,8192]{1,0:T(8,128)}, f32[32,32,64]{2,1,0:T(8,128)}, bf16[896,128]{1,0:T(8,128)(2,1)}, bf16[896,128]{1,0:T(8,128)(2,1)}) custom-call(s32[1,32]{1,0:T(1,128)} %get-tuple-element.21.refs_0_, s32[4,32]{1,0:T(4,128)} %bitcast.16, s32[1]{0:T(128)} %bitcast.place.refs_2_, bf16[32,8192]{1,0:T(8,128)(2,1)} %get-tuple-element.22.refs_1_.refs_3_, ...), custom_call_target="tpu_custom_call" | custom-call | flops 12000000000 | bytes 4000000 | tf_op jit(solution)/shard_map/edge/pallas_call | solution.py:455
  63.9 0.0 all-to-all-done.1
  63.9 7.5 %last.1 = f32[32,8192]{1,0:T(8,128)} custom-call(s32[1]{0:T(128)} %bitcast.place.refs_2_, bf16[16,512]{1,0:T(8,128)(2,1)} %get-tuple-element.25.refs_12_.low_siblings, bf16[128,128]{1,0:T(8,128)(2,1)S(1)} %bitcast.10, bf16[2,64,64]{2,1,0:T(8,128)(2,1)} %up.5, bf16[896,128]{1,0:T(8,128)(2,1)} %get-tuple-element.31.weights_high, ...), custom_call_target="tpu_custom_call" | custom-call | tf_op jit(solution)/shard_map/last/pallas_call | solution.py:491
Async XLA Ops:
  4.8 21.3 %all-to-all-start = ((bf16[16,16,128]{2,1,0:T(8,128)(2,1)}), bf16[16,16,128]{2,1,0:T(8,128)(2,1)S(1)}, u32[]{:S(2)}, u32[]{:S(2)}) async-start(bf16[16,16,128]{2,1,0:T(8,128)(2,1)} %get-tuple-element.20), calls=%async_computation | async-start | bytes 131072 | tf_op jit(solution)/shard_map/all_to_all | solution.py:400
  12.0 31.7 %collective-permute-start = (bf16[48,2048]{1,0:T(8,128)(2,1)}, bf16[48,2048]{1,0:T(8,128)(2,1)S(1)}, u32[]{:S(2)}, u32[]{:S(2)}) collective-permute-start(bf16[48,2048]{1,0:T(8,128)(2,1)} %get-tuple-element.28), channel_id=1, source_target_pairs={{0,4},{4,8},{8,12},{12,16},{16,20},{20,24},{24,28},{28,32},{32,36}... | collective-permute-start | bytes 589832 | tf_op jit(solution)/shard_map/ppermute | solution.py:401
  14.4 29.3 %collective-permute-start.1 = (bf16[48,2048]{1,0:T(8,128)(2,1)}, bf16[48,2048]{1,0:T(8,128)(2,1)S(1)}, u32[]{:S(2)}, u32[]{:S(2)}) collective-permute-start(bf16[48,2048]{1,0:T(8,128)(2,1)} %get-tuple-element.29), channel_id=1, source_target_pairs={{4,0},{8,4},{12,8},{16,12},{20,16},{24,20},{28,24},{32,28},{36,32}... | collective-permute-start | bytes 589832 | tf_op jit(solution)/shard_map/ppermute | solution.py:402
  28.1 35.8 %all-to-all-start.1 = ((bf16[8,16,128]{2,1,0:T(8,128)(2,1)}), bf16[8,16,128]{2,1,0:T(8,128)(2,1)S(1)}, u32[]{:S(2)}, u32[]{:S(2)}) async-start(bf16[8,16,128]{2,1,0:T(8,128)(2,1)} %get-tuple-element.26), calls=%async_computation.1 | async-start | bytes 65536 | tf_op jit(solution)/shard_map/all_to_all | solution.py:438
